TPU v7x, 512 devices: a whole 4x8x8 slice. The times are simulated.
512 devices in a mesh: ctx: 64 (over y, x, z_hi), dp: 8 (over z_lo, core).
Axes of the slice: x: 4, y: 8, z: 8 (z_hi: 2, z_lo: 4; z = z_hi * 4 + z_lo), core: 2. Of those that a mesh axis runs over, the one named last changes fastest.
Arguments:
- query_rows: bfloat16 [131072, 1024], P(('dp', 'ctx')), parts along dimension 0, may hold values from -100 to 100
- key_rows: bfloat16 [131072, 1024], P(('dp', 'ctx')), parts along dimension 0, may hold values from -5 to 5
- value_rows: bfloat16 [131072, 1024], P(('dp', 'ctx')), parts along dimension 0, may hold values from -6 to 6
- channels: bfloat16 [131072, 2048], P(('dp', 'ctx')), parts along dimension 0, may hold values from -6 to 6
- step_low: bfloat16 [131072, 128], P(('dp', 'ctx')), parts along dimension 0, may hold values from -6 to 6
- step_proj: bfloat16 [128, 2048], replicated, may hold values from -0.5 to 0.5
- step_bias: float32 [2048], replicated, may hold values from -8 to -2.5
- decay_log: float32 [16, 2048], replicated, may hold values from -6.5 to -0.5
- state_maps: float32 [2, 16, 131072], P(None, None, ('dp', 'ctx')), parts along dimension 2, may hold values from -6 to 6
- attend_weight: bfloat16 [1024, 128], replicated, may hold values from -0.5 to 0.5
- mixer_weight: bfloat16 [2048, 128], replicated, may hold values from -0.125 to 0.125
Outputs:
- token_vectors: bfloat16 [131072, 128], P(('dp', 'ctx')), parts along dimension 0
There are 8 independent parts, one for each index of `dp`. A program takes and returns all parts, laid end to end along the dimension named above; an argument that names none is the same for every part. Nothing has to cross between parts.
All inputs are finite; a program needn't handle non-finite values.
Results may differ from a plain program's by a relative error of at most 0.005.
Values may be sent and summed in bfloat16 or wider, within the bound.
No kernel may reach another device: no remote copies, remote signals or barrier semaphores. Data moves between devices by JAX's collectives and lax.ppermute only.
A program may use at most 128 MiB of HBM per device.

v0:
```python
import math

import jax
import jax.numpy as jnp
from jax import lax
from jax.sharding import PartitionSpec as P

HD = 128


def entering_2(part, axis, combine, identity):
    place = lax.axis_index(axis)
    gathered = jax.tree.map(lambda a: lax.all_gather(a, axis), part)
    state = jax.tree.map(lambda a, e: jnp.zeros_like(a) + jnp.asarray(e, a.dtype), part, identity)

    def one(hop, state):
        return combine(
            state, jax.tree.map(lambda a: lax.dynamic_index_in_dim(a, hop, 0, False), gathered)
        )

    return lax.fori_loop(0, place, one, state)


def from_behind(value, axis, steps):
    count = lax.axis_size(axis)
    initial, last = (max(0, -steps), min(count, count - steps))
    return lax.ppermute(value, axis, [(source, source + steps) for source in range(initial, last)])


def attention(query_rows, window, position):
    shard_rows, feature_count = query_rows.shape
    head_count = feature_count // HD
    window_rows = 4 * shard_rows
    query_block = query_rows.reshape(shard_rows, head_count, HD)
    key_block = window[0].reshape(5 * shard_rows, head_count, HD)
    value_block = window[1].reshape(5 * shard_rows, head_count, HD)
    scores = jnp.einsum(
        "qhd,khd->hqk", query_block, key_block, preferred_element_type=jnp.float32
    ) * (1.0 / math.sqrt(HD))
    query_pos = jnp.arange(shard_rows, dtype=jnp.int32)[:, None]
    column = jnp.arange(5 * shard_rows, dtype=jnp.int32)[None, :]
    offset = column - window_rows
    allowed = (
        (offset <= query_pos)
        & (query_pos - offset < window_rows)
        & (position * shard_rows + offset >= 0)
    )
    scores = jnp.where(allowed[None], scores, -1e30)
    row_max = jnp.max(scores, -1, keepdims=True)
    exp_terms = jnp.exp(scores - row_max)
    row_sum = jnp.sum(exp_terms, -1)
    weights = exp_terms.astype(jnp.bfloat16)
    summed = jnp.einsum("hqk,khd->qhd", weights, value_block, preferred_element_type=jnp.float32)
    result = summed / jnp.transpose(row_sum)[:, :, None]
    return result.reshape(shard_rows, feature_count).astype(jnp.bfloat16)


def run_mixer(carry_state, timestep, inflow, in_maps, out_maps, decay_rate, keep):
    shard_rows = timestep.shape[0]
    block_len = math.gcd(16, shard_rows)
    groups = shard_rows // block_len

    def advance(running, inputs):
        step_blk, inflow_blk, in_blk, out_blk = inputs
        collected = []
        for offset in range(block_len):
            running = (
                jnp.exp(step_blk[offset][None, :] * decay_rate) * running
                + in_blk[offset][:, None] * inflow_blk[offset][None, :]
            )
            if keep:
                collected.append(jnp.sum(out_blk[offset][:, None] * running, 0))
        if keep:
            return (running, jnp.stack(collected))
        return (running, jnp.zeros((block_len, 1), jnp.float32))

    final_state, outputs = lax.scan(
        advance,
        carry_state,
        (
            timestep.reshape(groups, block_len, -1),
            inflow.reshape(groups, block_len, -1),
            in_maps.reshape(groups, block_len, -1),
            out_maps.reshape(groups, block_len, -1),
        ),
    )
    return (final_state, outputs.reshape(shard_rows, -1))


def combine(earlier, following):
    return (earlier[0] * following[0], following[0] * earlier[1] + following[1])


def prefix_state(through, local_end):
    identity = (jnp.ones_like(through), jnp.zeros_like(local_end))
    result = entering_2((through, local_end), "ctx", combine, identity)
    return result[1]


def per_device(
    query_rows,
    key_rows,
    value_rows,
    channels,
    step_low,
    step_proj,
    step_bias,
    decay_log,
    state_maps,
    attend_weight,
    mixer_weight,
):
    position = lax.axis_index("ctx")
    stacked = jnp.stack([key_rows, value_rows])
    earlier = []
    moving = stacked
    for distance in range(1, 5):
        moving = from_behind(moving, "ctx", 1)
        earlier.append(moving)
    window = jnp.concatenate(earlier[::-1] + [stacked], 1)
    attended = attention(query_rows, window, position)
    timestep = jax.nn.softplus(
        jnp.dot(step_low, step_proj, preferred_element_type=jnp.float32) + step_bias
    )
    decay_rate = -jnp.exp(decay_log)
    inflow = timestep * channels.astype(jnp.float32)
    in_maps = jnp.transpose(state_maps[0])
    out_maps = jnp.transpose(state_maps[1])
    zero_state = jnp.zeros(decay_log.shape, jnp.float32)
    local_end, unused = run_mixer(
        zero_state, timestep, inflow, in_maps, out_maps, decay_rate, False
    )
    through = jnp.exp(decay_rate * jnp.sum(timestep, 0)[None, :])
    entering = prefix_state(through, local_end)
    final_state, outputs = run_mixer(
        entering, timestep, inflow, in_maps, out_maps, decay_rate, True
    )
    mixer_norm = (
        outputs * lax.rsqrt(jnp.mean(outputs * outputs, -1, keepdims=True) + 1e-05)
    ).astype(jnp.bfloat16)
    combined = jnp.dot(attended, attend_weight, preferred_element_type=jnp.float32) + jnp.dot(
        mixer_norm, mixer_weight, preferred_element_type=jnp.float32
    )
    return (combined * lax.rsqrt(jnp.mean(combined * combined, -1, keepdims=True) + 1e-06)).astype(
        jnp.bfloat16
    )


def solution(mesh):
    return jax.shard_map(
        per_device,
        mesh=mesh,
        in_specs=(
            P(("dp", "ctx"), None),
            P(("dp", "ctx"), None),
            P(("dp", "ctx"), None),
            P(("dp", "ctx"), None),
            P(("dp", "ctx"), None),
            P(),
            P(),
            P(),
            P(None, None, ("dp", "ctx")),
            P(),
            P(),
        ),
        out_specs=P(("dp", "ctx"), None),
        check_vma=False,
    )
```

profile of v0, /device:TPU:62, one launch (start us, length us, event | category | flops | bytes accessed | tf_op | source)
XLA Modules:
  0.0 732.6 jit_solution(15989149313683238210)
XLA Ops:
  6.5 4.4 convert_multiply_fusion
  11.8 42.9 %while.37 = (s32[]{:T(128)}, f32[16,2048]{1,0:T(8,128)S(1)}, f32[16,16,2048]{2,1,0:T(8,128)}, f32[16,2048]{1,0:T(8,128)S(1)}, f32[16,16,16]{2,1,0:T(8,128)S(1)},...) while((s32[]{:T(128)}, f32[16,2048]{1,0:T(8,128)S(1)}, ...), condition=%wide.region_4.5_spmd.clone, body=%wide.region_3.4_spmd.clone.sunk | while | flops 2129938 | bytes 1183251 | solution.py:77
  14.4 2.1 constant_dynamic-slice_fusion.115
  30.9 2.2 constant_dynamic-slice_fusion.115
  58.7 10.9 %collective-permute-start = (bf16[2,256,1024]{1,2,0:T(8,128)(2,1)S(1)}, bf16[2,256,1024]{1,2,0:T(8,128)(2,1)S(1)}, u32[]{:S(2)}, u32[]{:S(2)}) collective-permute-start(bf16[2,256,1024]{1,2,0:T(8,128)(2,1)S(1)} %pad_maximum_fusion), channel_id=1, source_target_pairs={{0,8},{8,16},{16,24},{24,32},{32,40},{40,48},{48,56},{56,64},{64,7... | collective-permute-start | bytes 3145736 | tf_op jit(solution)/shard_map/ppermute | solution.py:27
  69.6 51.9 %collective-permute-done = bf16[2,256,1024]{1,2,0:T(8,128)(2,1)S(1)} collective-permute-done((bf16[2,256,1024]{1,2,0:T(8,128)(2,1)S(1)}, bf16[2,256,1024]{1,2,0:T(8,128)(2,1)S(1)}, u32[]{:S(2)}, u32[]{:S(2)}) %collective-permute-start) | collective-permute-done | bytes 1048608 | tf_op jit(solution)/shard_map/ppermute | solution.py:27
  121.5 8.4 %collective-permute-start.1 = (bf16[2,256,1024]{1,2,0:T(8,128)(2,1)S(1)}, bf16[2,256,1024]{1,2,0:T(8,128)(2,1)S(1)}, u32[]{:S(2)}, u32[]{:S(2)}) collective-permute-start(bf16[2,256,1024]{1,2,0:T(8,128)(2,1)S(1)} %collective-permute-done), channel_id=1, source_target_pairs={{0,8},{8,16},{16,24},{24,32},{32,40},{40,48},{48,56},{56,64},{64,7... | collective-permute-start | bytes 3145736 | tf_op jit(solution)/shard_map/ppermute | solution.py:27
  129.9 28.1 %collective-permute-done.1 = bf16[2,256,1024]{1,2,0:T(8,128)(2,1)S(1)} collective-permute-done((bf16[2,256,1024]{1,2,0:T(8,128)(2,1)S(1)}, bf16[2,256,1024]{1,2,0:T(8,128)(2,1)S(1)}, u32[]{:S(2)}, u32[]{:S(2)}) %collective-permute-start.1) | collective-permute-done | bytes 1048608 | tf_op jit(solution)/shard_map/ppermute | solution.py:27
  159.0 5.8 collective-permute-start.2
  164.8 70.2 %collective-permute-done.2 = bf16[2,256,1024]{1,2,0:T(8,128)(2,1)} collective-permute-done((bf16[2,256,1024]{1,2,0:T(8,128)(2,1)S(1)}, bf16[2,256,1024]{1,2,0:T(8,128)(2,1)}, u32[]{:S(2)}, u32[]{:S(2)}) %collective-permute-start.2) | collective-permute-done | bytes 1048608 | tf_op jit(solution)/shard_map/ppermute | solution.py:27
  235.0 9.7 %collective-permute-start.3 = (bf16[2,256,1024]{1,2,0:T(8,128)(2,1)}, bf16[2,256,1024]{1,2,0:T(8,128)(2,1)}, u32[]{:S(2)}, u32[]{:S(2)}) collective-permute-start(bf16[2,256,1024]{1,2,0:T(8,128)(2,1)} %collective-permute-done.2), channel_id=1, source_target_pairs={{0,8},{8,16},{16,24},{24,32},{32,40},{40,48},{48,56},{56,64},{64,7... | collective-permute-start | bytes 3145736 | tf_op jit(solution)/shard_map/ppermute | solution.py:27
  246.5 90.6 %collective-permute-done.3 = bf16[2,256,1024]{1,2,0:T(8,128)(2,1)} collective-permute-done((bf16[2,256,1024]{1,2,0:T(8,128)(2,1)}, bf16[2,256,1024]{1,2,0:T(8,128)(2,1)}, u32[]{:S(2)}, u32[]{:S(2)}) %collective-permute-start.3) | collective-permute-done | bytes 1048608 | tf_op jit(solution)/shard_map/ppermute | solution.py:27
  345.5 3.6 divide_convert_fusion
  349.1 221.7 %all-gather.7.cloned.1.call-done = f32[1024,2048]{1,0:T(8,128)} async-done(((f32[16,2048]{1,0:T(8,128)}), f32[1024,2048]{1,0:T(8,128)}) %all-gather.7.cloned.1.call-update) | async-done | bytes 8388624 | tf_op jit(solution)/shard_map/all_gather | solution.py:13
  570.8 65.4 %while.35 = (s32[]{:T(128)}, f32[16,2048]{1,0:T(8,128)S(1)}, s32[]{:T(128)}, f32[64,16,2048]{2,1,0:T(8,128)}, f32[64,16,2048]{2,1,0:T(8,128)}, /*index=5*/s32[]{:T(128)}, s32[]{:T(128)}, s32[]{:T(128)}) while((s32[]{:T(128)}, f32[16,2048]{1,0:T(8,128)S(1)}, s32[]{:T(128)}, f32[64,16,2048]{2,1,0:T(8,128)}, f32[64,16,2048]{2,1,0:T(8,128)}, ...), condition=%wide.region_6.7_spmd, body=%wide.region_5.6_spmd.sunk | while | flops 65541 | bytes 524419 | solution.py:21
  636.2 85.6 %while.36 = (s32[]{:T(128)}, f32[16,2048]{1,0:T(8,128)S(1)}, f32[16,16,2048]{2,1,0:T(8,128)S(1)}, f32[16,16,2048]{2,1,0:T(8,128)}, f32[16,2048]{1,0:T(8,128)S(1)...) while((s32[]{:T(128)}, f32[16,2048]{1,0:T(8,128)S(1)}, ...), condition=%wide.region_24.25_spmd, body=%wide.region_7.24_spmd.sunk | while | flops 4685841 | bytes 3480861 | solution.py:77
  637.4 2.4 constant_dynamic-slice_fusion.114
  642.6 2.4 constant_dynamic-slice_fusion.114
  647.9 2.5 constant_dynamic-slice_fusion.114
  653.2 2.6 constant_dynamic-slice_fusion.114
  658.6 2.7 constant_dynamic-slice_fusion.114
  664.1 2.7 constant_dynamic-slice_fusion.114
  669.7 2.5 constant_dynamic-slice_fusion.114
  675.0 2.5 constant_dynamic-slice_fusion.114
  680.3 2.7 constant_dynamic-slice_fusion.114
  685.8 2.4 constant_dynamic-slice_fusion.114
  691.0 2.5 constant_dynamic-slice_fusion.114
  696.4 2.7 constant_dynamic-slice_fusion.114
  701.9 2.4 constant_dynamic-slice_fusion.114
  707.2 2.4 constant_dynamic-slice_fusion.114
  712.5 2.3 constant_dynamic-slice_fusion.114
  717.6 2.5 constant_dynamic-slice_fusion.114
  (297 shorter events, 166.1 us)
Async XLA Ops:
  6.5 334.7 %copy-start = (bf16[256,1024]{1,0:T(8,128)(2,1)S(1)}, bf16[256,1024]{1,0:T(8,128)(2,1)}, u32[]{:S(2)}) copy-start(bf16[256,1024]{1,0:T(8,128)(2,1)} %param.17) | copy-start | bytes 1572868
  6.5 4.4 copy-start.10
  6.5 5.2 copy-start.12
  6.5 342.5 %all-gather.5.cloned.1.call-start = ((), (), s32[]{:S(2)}) async-start(), calls=%async_computation | async-start | bytes 8519680 | tf_op jit(solution)/shard_map/all_gather | solution.py:13
  11.7 559.1 %all-gather.7.cloned.1.call-start = ((), (), s32[]{:S(2)}) async-start(), calls=%async_computation.1 | async-start | bytes 8519680 | tf_op jit(solution)/shard_map/all_gather | solution.py:13
  54.7 0.7 copy-start.11
  54.7 1.3 copy-start.7
  58.6 186.2 %copy-start.1 = (bf16[256,1024]{0,1:T(8,128)(2,1)}, bf16[256,1024]{0,1:T(8,128)(2,1)S(1)}, u32[]{:S(2)}) copy-start(bf16[256,1024]{0,1:T(8,128)(2,1)S(1)} %copy.18) | copy-start | bytes 1572868
  58.7 62.8 %collective-permute-start = (bf16[2,256,1024]{1,2,0:T(8,128)(2,1)S(1)}, bf16[2,256,1024]{1,2,0:T(8,128)(2,1)S(1)}, u32[]{:S(2)}, u32[]{:S(2)}) collective-permute-start(bf16[2,256,1024]{1,2,0:T(8,128)(2,1)S(1)} %pad_maximum_fusion), channel_id=1, source_target_pairs={{0,8},{8,16},{16,24},{24,32},{32,40},{40,48},{48,56},{56,64},{64,7... | collective-permute-start | bytes 3145736 | tf_op jit(solution)/shard_map/ppermute | solution.py:27
  121.5 123.2 %copy-start.3 = (bf16[2,256,1024]{1,2,0:T(8,128)(2,1)}, bf16[2,256,1024]{1,2,0:T(8,128)(2,1)S(1)}, u32[]{:S(2)}) copy-start(bf16[2,256,1024]{1,2,0:T(8,128)(2,1)S(1)} %collective-permute-done) | copy-start | bytes 3145732
  121.5 36.5 %collective-permute-start.1 = (bf16[2,256,1024]{1,2,0:T(8,128)(2,1)S(1)}, bf16[2,256,1024]{1,2,0:T(8,128)(2,1)S(1)}, u32[]{:S(2)}, u32[]{:S(2)}) collective-permute-start(bf16[2,256,1024]{1,2,0:T(8,128)(2,1)S(1)} %collective-permute-done), channel_id=1, source_target_pairs={{0,8},{8,16},{16,24},{24,32},{32,40},{40,48},{48,56},{56,64},{64,7... | collective-permute-start | bytes 3145736 | tf_op jit(solution)/shard_map/ppermute | solution.py:27
  158.0 1.0 copy-start.5
  159.0 76.0 %collective-permute-start.2 = (bf16[2,256,1024]{1,2,0:T(8,128)(2,1)S(1)}, bf16[2,256,1024]{1,2,0:T(8,128)(2,1)}, u32[]{:S(2)}, u32[]{:S(2)}) collective-permute-start(bf16[2,256,1024]{1,2,0:T(8,128)(2,1)S(1)} %collective-permute-done.1), channel_id=1, source_target_pairs={{0,8},{8,16},{16,24},{24,32},{32,40},{40,48},{48,56},{56,64},{64,7... | collective-permute-start | bytes 3145736 | tf_op jit(solution)/shard_map/ppermute | solution.py:27
  235.0 102.1 %collective-permute-start.3 = (bf16[2,256,1024]{1,2,0:T(8,128)(2,1)}, bf16[2,256,1024]{1,2,0:T(8,128)(2,1)}, u32[]{:S(2)}, u32[]{:S(2)}) collective-permute-start(bf16[2,256,1024]{1,2,0:T(8,128)(2,1)} %collective-permute-done.2), channel_id=1, source_target_pairs={{0,8},{8,16},{16,24},{24,32},{32,40},{40,48},{48,56},{56,64},{64,7... | collective-permute-start | bytes 3145736 | tf_op jit(solution)/shard_map/ppermute | solution.py:27
  245.5 94.2 %copy-start.6 = (bf16[2,256,1024]{1,2,0:T(8,128)(2,1)S(1)}, bf16[2,256,1024]{1,2,0:T(8,128)(2,1)}, u32[]{:S(2)}) copy-start(bf16[2,256,1024]{1,2,0:T(8,128)(2,1)} %copy-done.5) | copy-start | bytes 3145732
  338.4 1.5 copy-start.4
  339.8 1.1 copy-start.2
  722.0 1.7 copy-start.8
  722.1 1.1 copy-start.9
Sparse Core Ops, SparseCore 0:
  11.8 327.4 all-gather.4
  343.8 226.8 all-gather.6
where the time goes:
time: 738 us; the launch traced here: 733 us
  waiting for transfers between devices  463 us (63%)
  local copies, waits for them, and re-layouts  107 us (14%)
  other arithmetic  100 us (14%)
  starting transfers between devices  34.8 us (5%)
  between operations  13.7 us (2%)
  matrix products  11.8 us (2%)
    ppermute x4, waiting for transfers between devices, from_behind(): lax.ppermute(value, axis, [(source, source + steps) for source in range(i...  241 us
    all_gather x2, waiting for transfers between devices, entering_2(): gathered = jax.tree.map(lambda a: lax.all_gather(a, axis), part)  222 us
    slice x32, local copies, waits for them, and re-layouts, advance(): inflow_blk[offset][None, :]  72.1 us
    add x62, other arithmetic, combine(): return (earlier[0] * following[0], following[0] * earlier[1] + following[1])  64.2 us
    ppermute x4, starting transfers between devices, from_behind(): lax.ppermute(value, axis, [(source, source + steps) for source in range(i...  34.8 us
    reduce_sum x80, other arithmetic, advance(): collected.append(jnp.sum(out_blk[offset][:, None] * running, 0))  22.4 us
    mul x32, local copies, waits for them, and re-layouts, advance(): in_blk[offset][:, None] * inflow_blk[offset][None, :]  19.5 us
  transfers between devices with their start and end apart: 6, of which 5 were waited for; matrix products, arithmetic and copies ran while one was open for 8% of the time, Pallas kernels for 0%

commit v1 on v0

v1 whole, which is shorter than its diff:
```python
import math

import jax
import jax.numpy as jnp
from jax import lax
from jax.experimental import pallas as pl
from jax.experimental.pallas import tpu as pltpu
from jax.sharding import PartitionSpec as P

HD = 128
HEADS = 8
TOK = 256
NS = 16
CH = 2048
EMB = 128
CW = 512
LANES = 128
BLK = 16
N_CTX = 64
LOG2E = 1.4426950408889634
SCALE2 = LOG2E / math.sqrt(HD)
F32 = jnp.float32
BF16 = jnp.bfloat16


def dot(a, b):
    return jnp.dot(a, b, preferred_element_type=F32)


def dot_t(a, b):
    return lax.dot_general(a, b, (((1,), (1,)), ((), ())), preferred_element_type=F32)


def pieces(x):
    hi = x.astype(BF16)
    rest = x - hi.astype(F32)
    mid = rest.astype(BF16)
    low = (rest - mid.astype(F32)).astype(BF16)
    return hi, mid, low


def mixer_kernel(
    low_ref, proj_ref, bias_ref, chan_ref, log_ref, maps_ref,
    y_ref, cum_ref, send_ref, out_hi_ref, out_lo_ref,
    step_s, flow_s, in_s, hist,
):
    groups = CW // LANES

    @pl.when(pl.program_id(0) == 0)
    def _():
        in_map = maps_ref[0]
        for t in range(TOK):
            in_s[t] = jnp.broadcast_to(in_map[:, t : t + 1], (NS, LANES))
        spread = (
            lax.broadcasted_iota(jnp.int32, (NS, BLK * NS), 1) % NS
            == lax.broadcasted_iota(jnp.int32, (NS, BLK * NS), 0)
        ).astype(F32).astype(BF16)
        keep = (
            lax.broadcasted_iota(jnp.int32, (TOK, BLK * NS), 1) // NS
            == lax.broadcasted_iota(jnp.int32, (TOK, BLK * NS), 0) % BLK
        )
        hi, mid, _ = pieces(jnp.transpose(maps_ref[1]))
        out_hi_ref[...] = jnp.where(keep, dot(hi, spread), 0.0).astype(BF16)
        out_lo_ref[...] = jnp.where(keep, dot(mid, spread), 0.0).astype(BF16)

    step = jax.nn.softplus(dot(low_ref[...], proj_ref[...]) + bias_ref[...])
    step_s[...] = step.reshape(TOK // BLK, BLK, CW)
    flow_s[...] = (step * chan_ref[...].astype(F32)).reshape(TOK // BLK, BLK, CW)
    triangle = (
        lax.broadcasted_iota(jnp.int32, (TOK, TOK), 0)
        >= lax.broadcasted_iota(jnp.int32, (TOK, TOK), 1)
    ).astype(F32).astype(BF16)
    hi, mid, low = pieces(step)
    cum = dot(triangle, hi) + dot(triangle, mid) + dot(triangle, low)
    cum_ref[...] = cum.reshape(TOK // BLK, BLK, CW)
    rate = -jnp.exp(log_ref[...]) * LOG2E
    rates = [rate[:, g * LANES : (g + 1) * LANES] for g in range(groups)]

    def block(j, states):
        states = list(states)
        for t in range(BLK):
            gain = in_s[j * BLK + t]
            for g in range(groups):
                lanes = slice(g * LANES, (g + 1) * LANES)
                decay = jnp.exp2(step_s[j, t : t + 1, lanes] * rates[g])
                states[g] = decay * states[g] + gain * flow_s[j, t : t + 1, lanes]
                hist[t * NS : (t + 1) * NS, lanes] = states[g].astype(BF16)
        rows = pl.ds(pl.multiple_of(j * BLK, BLK), BLK)
        past = hist[...]
        y_ref[j] = dot(out_hi_ref[rows, :], past) + dot(out_lo_ref[rows, :], past)
        return tuple(states)

    states = lax.fori_loop(
        0, TOK // BLK, block, tuple(jnp.zeros((NS, LANES), F32) for _ in range(groups))
    )
    total = cum[TOK - 1 : TOK, :]
    hi, mid, low = (v.astype(F32) for v in pieces(total))
    for g in range(groups):
        lanes = slice(g * LANES, (g + 1) * LANES)
        for k in range(NS // 4):
            send_ref[g * 4 + k] = jnp.concatenate(
                [
                    states[g][4 * k : 4 * k + 4, :], hi[:, lanes], mid[:, lanes], low[:, lanes],
                    jnp.zeros((1, LANES), F32),
                ],
                0,
            ).astype(BF16)


def run_mixer(step_low, step_proj, step_bias, channels, decay_log, state_maps):
    blocked = (TOK // BLK, BLK, CW)
    whole = jax.ShapeDtypeStruct((TOK // BLK, BLK, CH), F32)
    square = jax.ShapeDtypeStruct((TOK, BLK * NS), BF16)
    fixed = lambda shape: pl.BlockSpec(shape, lambda i: (0,) * len(shape))
    return pl.pallas_call(
        mixer_kernel,
        grid=(CH // CW,),
        in_specs=[
            fixed((TOK, 128)),
            pl.BlockSpec((128, CW), lambda i: (0, i)),
            pl.BlockSpec((1, CW), lambda i: (0, i)),
            pl.BlockSpec((TOK, CW), lambda i: (0, i)),
            pl.BlockSpec((NS, CW), lambda i: (0, i)),
            fixed((2, NS, TOK)),
        ],
        out_specs=[
            pl.BlockSpec(blocked, lambda i: (0, 0, i)),
            pl.BlockSpec(blocked, lambda i: (0, 0, i)),
            pl.BlockSpec((CW // LANES * 4, 8, LANES), lambda i: (i, 0, 0)),
            fixed((TOK, BLK * NS)),
            fixed((TOK, BLK * NS)),
        ],
        out_shape=[whole, whole, jax.ShapeDtypeStruct((N_CTX, 8, LANES), BF16), square, square],
        scratch_shapes=[
            pltpu.VMEM(blocked, F32),
            pltpu.VMEM(blocked, F32),
            pltpu.VMEM((TOK, NS, LANES), F32),
            pltpu.VMEM((BLK * NS, CW), BF16),
        ],
        cost_estimate=pl.CostEstimate(
            flops=6_000_000_000, bytes_accessed=8 << 20, transcendentals=8 << 20
        ),
        name="mixer",
    )(step_low, step_proj, step_bias.reshape(1, CH), channels, decay_log, state_maps)


def prefix_kernel(pos_ref, got_ref, log_ref, out_ref):
    part = lax.rem(pos_ref[0], 4)
    rates = -jnp.exp(log_ref[...]) * LOG2E
    rate = rates[0:4]
    for k in range(1, 4):
        rate = jnp.where(part == k, rates[4 * k : 4 * k + 4], rate)
    state = jnp.zeros((4, LANES), F32)
    for s in range(N_CTX):
        out_ref[s] = state
        got = got_ref[s].astype(F32)
        total = got[4:5] + got[5:6] + got[6:7]
        state = jnp.exp2(rate * total) * state + got[0:4]


def run_prefix(position, got, decay_log):
    return pl.pallas_call(
        prefix_kernel,
        grid_spec=pltpu.PrefetchScalarGridSpec(
            num_scalar_prefetch=1,
            grid=(1,),
            in_specs=[
                pl.BlockSpec((N_CTX, 8, LANES), lambda i, pos: (0, 0, 0)),
                pl.BlockSpec((NS, LANES), lambda i, pos: (0, pos[0] // 4)),
            ],
            out_specs=pl.BlockSpec((N_CTX, 4, LANES), lambda i, pos: (0, 0, 0)),
        ),
        out_shape=jax.ShapeDtypeStruct((N_CTX, 4, LANES), F32),
        cost_estimate=pl.CostEstimate(flops=1 << 20, bytes_accessed=1 << 18, transcendentals=1 << 15),
        name="prefix",
    )(position, got, decay_log)


def finish_kernel(
    y_ref, cum_ref, enter_ref, log_ref, out_hi_ref, out_lo_ref, own_ref, back_ref, weight_ref,
    o_ref, hist, total_s,
):
    groups = CW // LANES
    i = pl.program_id(0)
    rate = -jnp.exp(log_ref[...]) * LOG2E
    rates = [rate[:, g * LANES : (g + 1) * LANES] for g in range(groups)]
    enter = [
        jnp.concatenate([enter_ref[g * 4 + k] for k in range(4)], 0) for g in range(groups)
    ]

    def block(j, carry):
        for t in range(BLK):
            for g in range(groups):
                lanes = slice(g * LANES, (g + 1) * LANES)
                decay = jnp.exp2(cum_ref[j, t : t + 1, lanes] * rates[g])
                hist[t * NS : (t + 1) * NS, lanes] = (decay * enter[g]).astype(BF16)
        rows = pl.ds(pl.multiple_of(j * BLK, BLK), BLK)
        past = hist[...]
        total_s[i, rows, :] = (
            y_ref[j] + dot(out_hi_ref[rows, :], past) + dot(out_lo_ref[rows, :], past)
        )
        return carry

    lax.fori_loop(0, TOK // BLK, block, 0)

    @pl.when(i == CH // CW - 1)
    def _():
        square = jnp.zeros((TOK, 1), F32)
        for k in range(CH // CW):
            square += jnp.sum(total_s[k] * total_s[k], -1, keepdims=True)
        inverse = lax.rsqrt(square * (1.0 / CH) + 1e-05)
        combined = own_ref[...] + back_ref[...].astype(F32)
        for k in range(CH // CW):
            combined += dot(
                (total_s[k] * inverse).astype(BF16), weight_ref[k * CW : (k + 1) * CW, :]
            )
        mean = jnp.mean(combined * combined, -1, keepdims=True)
        o_ref[...] = (combined * lax.rsqrt(mean + 1e-06)).astype(BF16)


def run_finish(y, cum, enter, decay_log, out_hi, out_lo, own, back, mixer_weight):
    blocked = pl.BlockSpec((TOK // BLK, BLK, CW), lambda i: (0, 0, i))
    fixed = lambda shape: pl.BlockSpec(shape, lambda i: (0,) * len(shape))
    return pl.pallas_call(
        finish_kernel,
        grid=(CH // CW,),
        in_specs=[
            blocked,
            blocked,
            pl.BlockSpec((CW // LANES * 4, 4, LANES), lambda i: (i, 0, 0)),
            pl.BlockSpec((NS, CW), lambda i: (0, i)),
            fixed((TOK, BLK * NS)),
            fixed((TOK, BLK * NS)),
            fixed((TOK, EMB)),
            fixed((TOK, EMB)),
            fixed((CH, EMB)),
        ],
        out_specs=fixed((TOK, EMB)),
        out_shape=jax.ShapeDtypeStruct((TOK, EMB), BF16),
        scratch_shapes=[
            pltpu.VMEM((BLK * NS, CW), BF16),
            pltpu.VMEM((CH // CW, TOK, CW), F32),
        ],
        cost_estimate=pl.CostEstimate(
            flops=4_000_000_000, bytes_accessed=6 << 20, transcendentals=8 << 20
        ),
        name="finish",
    )(y, cum, enter, decay_log, out_hi, out_lo, own, back, mixer_weight)


def scores_kernel(pos_ref, q_ref, p_ref, k0_ref, k1_ref, k2_ref, w_ref, stat_ref, table):
    h = pl.program_id(0)
    side = lax.rem(pos_ref[0], 2)
    pair = pos_ref[0] // 2
    gone1 = jnp.where(pair >= 1, 0.0, -1e30).astype(F32)
    gone2 = jnp.where(pair >= 2, 0.0, -1e30).astype(F32)
    row = lax.broadcasted_iota(jnp.int32, (TOK, TOK), 0)
    column = lax.broadcasted_iota(jnp.int32, (TOK, TOK), 1)
    lane = lax.broadcasted_iota(jnp.int32, (TOK, LANES), 1)
    k0, k1, k2 = k0_ref[...], k1_ref[...], k2_ref[...]

    @pl.when(h == 0)
    def _():
        table[...] = jnp.zeros_like(table)

    def weigh(blocks, first, slot):
        top = blocks[0][1] + jnp.max(blocks[0][0], -1, keepdims=True)
        for score, gone in blocks[1:]:
            top = jnp.maximum(top, gone + jnp.max(score, -1, keepdims=True))
        total = jnp.zeros((TOK, 1), F32)
        for n, (score, gone) in enumerate(blocks):
            terms = jnp.exp2(score - (top - gone))
            total += jnp.sum(terms, -1, keepdims=True)
            w_ref[0, :, (first + n) * TOK : (first + n + 1) * TOK] = terms.astype(BF16)
        now = table[...]
        now = jnp.where(lane == slot + h, top, now)
        table[...] = jnp.where(lane == slot + HEADS + h, total, now)

    q = q_ref[...]
    weigh(
        [
            (jnp.where(column <= row, dot_t(q, k0) * SCALE2, -1e30), jnp.float32(0.0)),
            (dot_t(q, k1) * SCALE2, gone1),
            (jnp.where(column > row, dot_t(q, k2) * SCALE2, -1e30), gone2),
        ],
        0,
        0,
    )
    other = p_ref[...]
    ka = jnp.where(side == 0, k0, k1)
    kb = jnp.where(side == 0, k1, k2)
    weigh(
        [
            (dot_t(other, ka) * SCALE2, jnp.where(side == 0, 0.0, gone1)),
            (dot_t(other, kb) * SCALE2, jnp.where(side == 0, gone1, gone2)),
        ],
        3,
        2 * HEADS,
    )

    @pl.when(h == HEADS - 1)
    def _():
        stat_ref[...] = jnp.transpose(table[...])[: 4 * HEADS, :]


def run_scores(position, query, other, k0, k1, k2):
    head = pl.BlockSpec((TOK, HD), lambda h, pos: (0, h))
    return pl.pallas_call(
        scores_kernel,
        grid_spec=pltpu.PrefetchScalarGridSpec(
            num_scalar_prefetch=1,
            grid=(HEADS,),
            in_specs=[head] * 5,
            out_specs=[
                pl.BlockSpec((1, TOK, 5 * TOK), lambda h, pos: (h, 0, 0)),
                pl.BlockSpec((4 * HEADS, TOK), lambda h, pos: (0, 0)),
            ],
            scratch_shapes=[pltpu.VMEM((TOK, LANES), F32)],
        ),
        out_shape=[
            jax.ShapeDtypeStruct((HEADS, TOK, 5 * TOK), BF16),
            jax.ShapeDtypeStruct((4 * HEADS, TOK), F32),
        ],
        cost_estimate=pl.CostEstimate(
            flops=700_000_000, bytes_accessed=8 << 20, transcendentals=3 << 20
        ),
        name="scores",
    )(position, query, other, k0, k1, k2)


def values_kernel(
    pos_ref, w_ref, v0_ref, v1_ref, v2_ref, mine_ref, got_ref, weight_ref,
    own_ref, give_ref, scale_own, scale_other,
):
    h = pl.program_id(0)
    side = lax.rem(pos_ref[0], 2)
    lane = lax.broadcasted_iota(jnp.int32, (TOK, LANES), 1)

    @pl.when(h == 0)
    def _():
        def scales(here, there):
            (m0, l0), (m1, l1) = here, there
            top = jnp.maximum(m0, m1)
            f0 = jnp.exp2(m0 - top)
            scale = f0 / (l0 * f0 + l1 * jnp.exp2(m1 - top))
            return jnp.transpose(
                jnp.concatenate([scale, jnp.zeros((LANES - HEADS, TOK), F32)], 0)
            )

        at = lambda ref, k: (ref[k * 8 : k * 8 + 8, :], ref[k * 8 + 8 : k * 8 + 16, :])
        scale_own[...] = scales(at(mine_ref, 0), at(got_ref, 2))
        scale_other[...] = scales(at(mine_ref, 2), at(got_ref, 0))
        own_ref[...] = jnp.zeros_like(own_ref)
        give_ref[...] = jnp.zeros_like(give_ref)

    column = lambda ref: jnp.sum(jnp.where(lane == h, ref[...], 0.0), -1, keepdims=True)
    v0, v1, v2 = v0_ref[...], v1_ref[...], v2_ref[...]
    w = lambda n: w_ref[0, :, n * TOK : (n + 1) * TOK]
    mine = dot(w(0), v0) + dot(w(1), v1) + dot(w(2), v2)
    other = dot(w(3), jnp.where(side == 0, v0, v1)) + dot(w(4), jnp.where(side == 0, v1, v2))
    own_ref[...] += dot((mine * column(scale_own)).astype(BF16), weight_ref[...])
    give_ref[...] += dot((other * column(scale_other)).astype(BF16), weight_ref[...])


def run_values(position, weights, v0, v1, v2, mine, got, attend_weight):
    head = pl.BlockSpec((TOK, HD), lambda h, pos: (0, h))
    fixed = lambda shape: pl.BlockSpec(shape, lambda h, pos: (0,) * len(shape))
    return pl.pallas_call(
        values_kernel,
        grid_spec=pltpu.PrefetchScalarGridSpec(
            num_scalar_prefetch=1,
            grid=(HEADS,),
            in_specs=[
                pl.BlockSpec((1, TOK, 5 * TOK), lambda h, pos: (h, 0, 0)),
                head, head, head,
                fixed((4 * HEADS, TOK)),
                fixed((4 * HEADS, TOK)),
                pl.BlockSpec((HD, EMB), lambda h, pos: (h, 0)),
            ],
            out_specs=[fixed((TOK, EMB)), fixed((TOK, EMB))],
            scratch_shapes=[pltpu.VMEM((TOK, LANES), F32)] * 2,
        ),
        out_shape=[jax.ShapeDtypeStruct((TOK, EMB), F32)] * 2,
        cost_estimate=pl.CostEstimate(
            flops=700_000_000, bytes_accessed=8 << 20, transcendentals=1 << 12
        ),
        name="values",
    )(position, weights, v0, v1, v2, mine, got, attend_weight)


def shift(value, steps):
    return lax.ppermute(value, "ctx", [(s, s + steps) for s in range(N_CTX - steps)])


def swap(value):
    return lax.ppermute(value, "ctx", [(s, s ^ 1) for s in range(N_CTX)])


def per_device(
    query_rows, key_rows, value_rows, channels, step_low, step_proj, step_bias, decay_log,
    state_maps, attend_weight, mixer_weight,
):
    position = lax.axis_index("ctx").astype(jnp.int32).reshape(1)
    k1 = shift(key_rows, 2)
    other = swap(query_rows)
    k2 = shift(key_rows, 4)
    v1 = shift(value_rows, 2)
    v2 = shift(value_rows, 4)

    y, cum, send, out_hi, out_lo = run_mixer(
        step_low, step_proj, step_bias, channels, decay_log, state_maps
    )
    got = lax.all_to_all(send, "ctx", 0, 0, tiled=True)
    given = run_prefix(position, got, decay_log)
    enter = lax.all_to_all(given, "ctx", 0, 0, tiled=True)

    weights, stats = run_scores(position, query_rows, other, key_rows, k1, k2)
    got_stats = swap(stats)
    own, give = run_values(position, weights, value_rows, v1, v2, stats, got_stats, attend_weight)
    back = swap(give.astype(BF16))
    return run_finish(y, cum, enter, decay_log, out_hi, out_lo, own, back, mixer_weight)


def solution(mesh):
    rows = P(("dp", "ctx"), None)
    return jax.shard_map(
        per_device,
        mesh=mesh,
        in_specs=(rows, rows, rows, rows, rows, P(), P(), P(), P(None, None, ("dp", "ctx")), P(), P()),
        out_specs=rows,
        check_vma=False,
    )
```

time: 738 us -> 149 us (0.20)
  the two profiles are of different devices: /device:TPU:62 before, /device:TPU:2 now
where the time goes in v1:
time: 149 us; the launch traced here: 148 us
  Pallas kernels  64.7 us (43%)
  starting transfers between devices  56.7 us (38%)
  waiting for transfers between devices  21.6 us (14%)
  local copies, waits for them, and re-layouts  3.67 us (2%)
    pallas_call x1, Pallas kernels, run_mixer(): pl.pallas_call(mixer_kernel, grid=(CH // CW,), in_specs=[fixed((TOK, 128)...  26.3 us
    ppermute x3, starting transfers between devices, swap(): return lax.ppermute(value, 'ctx', [(s, s ^ 1) for s in range(N_CTX)])  25.5 us
    pallas_call x1, Pallas kernels, run_finish(): pl.pallas_call(finish_kernel, grid=(CH // CW,), in_specs=[blocked, blocke...  19.6 us
    all_to_all x1, waiting for transfers between devices, per_device(): got = lax.all_to_all(send, 'ctx', 0, 0, tiled=True)  16.1 us
    ppermute x4, starting transfers between devices, shift(): lax.ppermute(value, 'ctx', [(s, s + steps) for s in range(N_CTX - steps)])  15.5 us
    pallas_call x1, Pallas kernels, run_scores(): pl.pallas_call(scores_kernel, grid_spec=pltpu.PrefetchScalarGridSpec(num_...  9.04 us
    all_to_all x1, starting transfers between devices, per_device(): got = lax.all_to_all(send, 'ctx', 0, 0, tiled=True)  8.21 us
    pallas_call x1, Pallas kernels, run_values(): pl.pallas_call(values_kernel, grid_spec=pltpu.PrefetchScalarGridSpec(num_...  8.03 us
  transfers between devices with their start and end apart: 9, of which 3 were waited for; matrix products, arithmetic and copies ran while one was open for 1% of the time, Pallas kernels for 31%

profile of v1, /device:TPU:2, one launch (start us, length us, event | category | flops | bytes accessed | tf_op | source)
XLA Modules:
  0.0 147.7 jit_solution(10854000284641732002)
XLA Ops:
  0.0 3.4 %collective-permute-start.1 = (bf16[256,1024]{1,0:T(8,128)(2,1)}, bf16[256,1024]{1,0:T(8,128)(2,1)S(1)}, u32[]{:S(2)}, u32[]{:S(2)}) collective-permute-start(bf16[256,1024]{1,0:T(8,128)(2,1)} %k0_ref.1), channel_id=1, source_target_pairs={{0,16},{8,24},{16,32},{24,40},{32,48},{40,56},{48,64},{56,72},{64,... | collective-permute-start | bytes 1572872 | tf_op jit(solution)/shard_map/ppermute | solution.py:392
  3.4 4.1 %collective-permute-start.2 = (bf16[256,1024]{1,0:T(8,128)(2,1)}, bf16[256,1024]{1,0:T(8,128)(2,1)S(1)}, u32[]{:S(2)}, u32[]{:S(2)}) collective-permute-start(bf16[256,1024]{1,0:T(8,128)(2,1)} %k0_ref.1), channel_id=1, source_target_pairs={{0,32},{8,40},{16,48},{24,56},{32,64},{40,72},{48,80},{56,88},{64,... | collective-permute-start | bytes 1572872 | tf_op jit(solution)/shard_map/ppermute | solution.py:392
  7.5 2.8 %collective-permute-start.3 = (bf16[256,1024]{1,0:T(8,128)(2,1)}, bf16[256,1024]{1,0:T(8,128)(2,1)S(1)}, u32[]{:S(2)}, u32[]{:S(2)}) collective-permute-start(bf16[256,1024]{1,0:T(8,128)(2,1)} %v0_ref.1), channel_id=1, source_target_pairs={{0,16},{8,24},{16,32},{24,40},{32,48},{40,56},{48,64},{56,72},{64,... | collective-permute-start | bytes 1572872 | tf_op jit(solution)/shard_map/ppermute | solution.py:392
  10.2 5.3 %collective-permute-start.4 = (bf16[256,1024]{1,0:T(8,128)(2,1)}, bf16[256,1024]{1,0:T(8,128)(2,1)S(1)}, u32[]{:S(2)}, u32[]{:S(2)}) collective-permute-start(bf16[256,1024]{1,0:T(8,128)(2,1)} %v0_ref.1), channel_id=1, source_target_pairs={{0,32},{8,40},{16,48},{24,56},{32,64},{40,72},{48,80},{56,88},{64,... | collective-permute-start | bytes 1572872 | tf_op jit(solution)/shard_map/ppermute | solution.py:392
  15.5 10.9 %collective-permute-start = (bf16[256,1024]{1,0:T(8,128)(2,1)}, bf16[256,1024]{1,0:T(8,128)(2,1)S(1)}, u32[]{:S(2)}, u32[]{:S(2)}) collective-permute-start(bf16[256,1024]{1,0:T(8,128)(2,1)} %q_ref.1), channel_id=1, source_target_pairs={{0,8},{8,0},{16,24},{24,16},{32,40},{40,32},{48,56},{56,48},{64,72... | collective-permute-start | bytes 1572872 | tf_op jit(solution)/shard_map/ppermute | solution.py:396
  26.5 26.3 %mixer.1 = (f32[16,16,2048]{2,1,0:T(8,128)}, f32[16,16,2048]{2,1,0:T(8,128)}, bf16[64,8,128]{2,1,0:T(8,128)(2,1)}, bf16[256,256]{1,0:T(8,128)(2,1)}, bf16[256,256]{1,0:T(8,128)(2,1)}) custom-call(bf16[256,128]{1,0:T(8,128)(2,1)} %low_ref.1, bf16[128,2048]{1,0:T(8,128)(2,1)} %proj_ref.1, f32[1,2048]{1,0:T(1,128)} %bitcast.2, bf16[256,2048]{1,0:T(8,128)(2,1)} %chan_ref.1, ...), custom_call_target="tpu_custom_call" | custom-call | flops 6000000000 | bytes 8388608 | tf_op jit(solution)/shard_map/mixer/pallas_call | solution.py:115
  52.8 8.2 %all-to-all-start = ((bf16[64,8,128]{2,1,0:T(8,128)(2,1)}), bf16[64,8,128]{2,1,0:T(8,128)(2,1)S(1)}, u32[]{:S(2)}, u32[]{:S(2)}) async-start(bf16[64,8,128]{2,1,0:T(8,128)(2,1)} %get-tuple-element.16), calls=%async_computation | async-start | bytes 262144 | tf_op jit(solution)/shard_map/all_to_all | solution.py:413
  61.0 16.1 %all-to-all-done.got_ref = bf16[64,8,128]{2,1,0:T(8,128)(2,1)S(1)} async-done(((bf16[64,8,128]{2,1,0:T(8,128)(2,1)}), bf16[64,8,128]{2,1,0:T(8,128)(2,1)S(1)}, u32[]{:S(2)}, u32[]{:S(2)}) %all-to-all-start) | async-done | bytes 131104 | tf_op jit(solution)/shard_map/all_to_all | solution.py:413
  77.1 0.7 copy-done.2
  77.8 1.7 %prefix.1 = f32[64,4,128]{2,1,0:T(4,128)} custom-call(s32[1]{0:T(128)} %bitcast.1.pos_ref, bf16[64,8,128]{2,1,0:T(8,128)(2,1)} %copy-done.2, f32[16,2048]{1,0:T(8,128)} %log_ref.5), custom_call_target="tpu_custom_call" | custom-call | flops 1048576 | bytes 262144 | tf_op jit(solution)/shard_map/prefix/pallas_call | solution.py:162
  79.5 7.5 %all-to-all-start.1 = ((f32[64,4,128]{2,1,0:T(4,128)}), f32[64,4,128]{2,1,0:T(4,128)S(1)}, u32[]{:S(2)}, u32[]{:S(2)}) async-start(f32[64,4,128]{2,1,0:T(4,128)} %prefix.1), calls=%async_computation.1 | async-start | bytes 262144 | tf_op jit(solution)/shard_map/all_to_all | solution.py:415
  87.0 0.0 collective-permute-done.p_ref
  87.0 0.0 collective-permute-done.1.k1_ref
  87.0 0.0 copy-start.5
  87.0 0.0 collective-permute-done.2.k2_ref
  87.1 0.8 copy-done.7
  87.8 0.2 copy-done.5
  88.0 0.8 copy-done.6
  88.8 9.0 %scores.1 = (bf16[8,256,1280]{2,1,0:T(8,128)(2,1)}, f32[32,256]{1,0:T(8,128)}) custom-call(s32[1]{0:T(128)} %bitcast.1.pos_ref, bf16[256,1024]{1,0:T(8,128)(2,1)} %q_ref.1, bf16[256,1024]{1,0:T(8,128)(2,1)} %copy-done.7, bf16[256,1024]{1,0:T(8,128)(2,1)} %k0_ref.1, bf16[256,1024]{1,0:T(8,128)(2,1)} %copy-done.5, bf16[256,1024]{1,0:T(8,128)(2,1)} %copy-done.6), custom_call_target="tpu_custom_call" | custom-call | flops 700000000 | bytes 8388608 | tf_op jit(solution)/shard_map/scores/pallas_call | solution.py:308
  97.8 7.3 %collective-permute-start.5 = (f32[32,256]{1,0:T(8,128)}, f32[32,256]{1,0:T(8,128)S(1)}, u32[]{:S(2)}, u32[]{:S(2)}) collective-permute-start(f32[32,256]{1,0:T(8,128)} %get-tuple-element.20.mine_ref), channel_id=1, source_target_pairs={{0,8},{8,0},{16,24},{24,16},{32,40},{40,32},{48,56},{56,48},{64,72... | collective-permute-start | bytes 98312 | tf_op jit(solution)/shard_map/ppermute | solution.py:396
  105.1 0.0 collective-permute-done.3.v1_ref
  105.1 0.0 copy-start
  105.1 0.0 collective-permute-done.4.v2_ref
  105.2 2.7 %collective-permute-done.5.got_ref = f32[32,256]{1,0:T(8,128)S(1)} collective-permute-done((f32[32,256]{1,0:T(8,128)}, f32[32,256]{1,0:T(8,128)S(1)}, u32[]{:S(2)}, u32[]{:S(2)}) %collective-permute-start.5) | collective-permute-done | bytes 32800 | tf_op jit(solution)/shard_map/ppermute | solution.py:396
  107.9 0.6 copy-done.4
  108.5 8.0 %values.1 = (f32[256,128]{1,0:T(8,128)}, f32[256,128]{1,0:T(8,128)}) custom-call(s32[1]{0:T(128)} %bitcast.1.pos_ref, bf16[8,256,1280]{2,1,0:T(8,128)(2,1)} %get-tuple-element.19.w_ref, bf16[256,1024]{1,0:T(8,128)(2,1)} %v0_ref.1, bf16[256,1024]{1,0:T(8,128)(2,1)} %copy-done, bf16[256,1024]{1,0:T(8,128)(2,1)} %copy-done.1, ...), custom_call_target="tpu_custom_call" | custom-call | flops 700000000 | bytes 8388608 | tf_op jit(solution)/shard_map/values/pallas_call | solution.py:368
  116.5 0.9 convert_element_type.3
  117.4 7.3 %collective-permute-start.6 = (bf16[256,128]{1,0:T(8,128)(2,1)S(1)}, bf16[256,128]{1,0:T(8,128)(2,1)S(1)}, u32[]{:S(2)}, u32[]{:S(2)}) collective-permute-start(bf16[256,128]{1,0:T(8,128)(2,1)S(1)} %convert_element_type.3), channel_id=1, source_target_pairs={{0,8},{8,0},{16,24},{24,16},{32,40},{40,32},{48,56},{56,48},{64,72... | collective-permute-start | bytes 196616 | tf_op jit(solution)/shard_map/ppermute | solution.py:396
  124.7 0.0 all-to-all-done.1.enter_ref
  124.7 2.8 %collective-permute-done.6.back_ref = bf16[256,128]{1,0:T(8,128)(2,1)S(1)} collective-permute-done((bf16[256,128]{1,0:T(8,128)(2,1)S(1)}, bf16[256,128]{1,0:T(8,128)(2,1)S(1)}, u32[]{:S(2)}, u32[]{:S(2)}) %collective-permute-start.6) | collective-permute-done | bytes 65568 | tf_op jit(solution)/shard_map/ppermute | solution.py:396
  127.5 0.6 copy-done.8
  128.2 19.6 %finish.1 = bf16[256,128]{1,0:T(8,128)(2,1)} custom-call(f32[16,16,2048]{2,1,0:T(8,128)} %get-tuple-element.14.y_ref, f32[16,16,2048]{2,1,0:T(8,128)} %get-tuple-element.15.cum_ref, f32[64,4,128]{2,1,0:T(4,128)} %copy-done.3, f32[16,2048]{1,0:T(8,128)} %log_ref.5, bf16[256,256]{1,0:T(8,128)(2,1)} %get-tuple-element.17.out_hi_ref, ...), custom_call_target="tpu_custom_call" | custom-call | flops 4000000000 | bytes 6291456 | tf_op jit(solution)/shard_map/finish/pallas_call | solution.py:224
  (10 shorter events, 0.0 us)
Async XLA Ops:
  0.0 87.0 %collective-permute-start.1 = (bf16[256,1024]{1,0:T(8,128)(2,1)}, bf16[256,1024]{1,0:T(8,128)(2,1)S(1)}, u32[]{:S(2)}, u32[]{:S(2)}) collective-permute-start(bf16[256,1024]{1,0:T(8,128)(2,1)} %k0_ref.1), channel_id=1, source_target_pairs={{0,16},{8,24},{16,32},{24,40},{32,48},{40,56},{48,64},{56,72},{64,... | collective-permute-start | bytes 1572872 | tf_op jit(solution)/shard_map/ppermute | solution.py:392
  3.4 83.6 %collective-permute-start.2 = (bf16[256,1024]{1,0:T(8,128)(2,1)}, bf16[256,1024]{1,0:T(8,128)(2,1)S(1)}, u32[]{:S(2)}, u32[]{:S(2)}) collective-permute-start(bf16[256,1024]{1,0:T(8,128)(2,1)} %k0_ref.1), channel_id=1, source_target_pairs={{0,32},{8,40},{16,48},{24,56},{32,64},{40,72},{48,80},{56,88},{64,... | collective-permute-start | bytes 1572872 | tf_op jit(solution)/shard_map/ppermute | solution.py:392
  7.5 97.7 %collective-permute-start.3 = (bf16[256,1024]{1,0:T(8,128)(2,1)}, bf16[256,1024]{1,0:T(8,128)(2,1)S(1)}, u32[]{:S(2)}, u32[]{:S(2)}) collective-permute-start(bf16[256,1024]{1,0:T(8,128)(2,1)} %v0_ref.1), channel_id=1, source_target_pairs={{0,16},{8,24},{16,32},{24,40},{32,48},{40,56},{48,64},{56,72},{64,... | collective-permute-start | bytes 1572872 | tf_op jit(solution)/shard_map/ppermute | solution.py:392
  10.2 94.9 %collective-permute-start.4 = (bf16[256,1024]{1,0:T(8,128)(2,1)}, bf16[256,1024]{1,0:T(8,128)(2,1)S(1)}, u32[]{:S(2)}, u32[]{:S(2)}) collective-permute-start(bf16[256,1024]{1,0:T(8,128)(2,1)} %v0_ref.1), channel_id=1, source_target_pairs={{0,32},{8,40},{16,48},{24,56},{32,64},{40,72},{48,80},{56,88},{64,... | collective-permute-start | bytes 1572872 | tf_op jit(solution)/shard_map/ppermute | solution.py:392
  15.5 71.5 %collective-permute-start = (bf16[256,1024]{1,0:T(8,128)(2,1)}, bf16[256,1024]{1,0:T(8,128)(2,1)S(1)}, u32[]{:S(2)}, u32[]{:S(2)}) collective-permute-start(bf16[256,1024]{1,0:T(8,128)(2,1)} %q_ref.1), channel_id=1, source_target_pairs={{0,8},{8,0},{16,24},{24,16},{32,40},{40,32},{48,56},{56,48},{64,72... | collective-permute-start | bytes 1572872 | tf_op jit(solution)/shard_map/ppermute | solution.py:396
  52.8 24.3 %all-to-all-start = ((bf16[64,8,128]{2,1,0:T(8,128)(2,1)}), bf16[64,8,128]{2,1,0:T(8,128)(2,1)S(1)}, u32[]{:S(2)}, u32[]{:S(2)}) async-start(bf16[64,8,128]{2,1,0:T(8,128)(2,1)} %get-tuple-element.16), calls=%async_computation | async-start | bytes 262144 | tf_op jit(solution)/shard_map/all_to_all | solution.py:413
  77.1 0.7 copy-start.2
  79.5 45.2 %all-to-all-start.1 = ((f32[64,4,128]{2,1,0:T(4,128)}), f32[64,4,128]{2,1,0:T(4,128)S(1)}, u32[]{:S(2)}, u32[]{:S(2)}) async-start(f32[64,4,128]{2,1,0:T(4,128)} %prefix.1), calls=%async_computation.1 | async-start | bytes 262144 | tf_op jit(solution)/shard_map/all_to_all | solution.py:415
  87.0 0.8 copy-start.7
  87.0 1.0 copy-start.5
  88.0 0.8 copy-start.6
  97.8 10.0 %collective-permute-start.5 = (f32[32,256]{1,0:T(8,128)}, f32[32,256]{1,0:T(8,128)S(1)}, u32[]{:S(2)}, u32[]{:S(2)}) collective-permute-start(f32[32,256]{1,0:T(8,128)} %get-tuple-element.20.mine_ref), channel_id=1, source_target_pairs={{0,8},{8,0},{16,24},{24,16},{32,40},{40,32},{48,56},{56,48},{64,72... | collective-permute-start | bytes 98312 | tf_op jit(solution)/shard_map/ppermute | solution.py:396
  105.1 2.7 %copy-start = (bf16[256,1024]{1,0:T(8,128)(2,1)}, bf16[256,1024]{1,0:T(8,128)(2,1)S(1)}, u32[]{:S(2)}) copy-start(bf16[256,1024]{1,0:T(8,128)(2,1)S(1)} %collective-permute-done.3.v1_ref) | copy-start | bytes 1572868
  105.2 2.7 %copy-start.1 = (bf16[256,1024]{1,0:T(8,128)(2,1)}, bf16[256,1024]{1,0:T(8,128)(2,1)S(1)}, u32[]{:S(2)}) copy-start(bf16[256,1024]{1,0:T(8,128)(2,1)S(1)} %collective-permute-done.4.v2_ref) | copy-start | bytes 1572868
  107.9 0.6 copy-start.4
  117.4 10.1 %collective-permute-start.6 = (bf16[256,128]{1,0:T(8,128)(2,1)S(1)}, bf16[256,128]{1,0:T(8,128)(2,1)S(1)}, u32[]{:S(2)}, u32[]{:S(2)}) collective-permute-start(bf16[256,128]{1,0:T(8,128)(2,1)S(1)} %convert_element_type.3), channel_id=1, source_target_pairs={{0,8},{8,0},{16,24},{24,16},{32,40},{40,32},{48,56},{56,48},{64,72... | collective-permute-start | bytes 196616 | tf_op jit(solution)/shard_map/ppermute | solution.py:396
  124.7 2.8 %copy-start.3 = (f32[64,4,128]{2,1,0:T(4,128)}, f32[64,4,128]{2,1,0:T(4,128)S(1)}, u32[]{:S(2)}) copy-start(f32[64,4,128]{2,1,0:T(4,128)S(1)} %all-to-all-done.1.enter_ref) | copy-start | bytes 393220
  127.5 0.6 copy-start.8

commit v2 on v1

v2 whole, which is shorter than its diff:
```python
import functools
import math

import jax
import jax.numpy as jnp
from jax import lax
from jax.experimental import pallas as pl
from jax.experimental.pallas import tpu as pltpu
from jax.sharding import PartitionSpec as P


HD = 128
HEADS = 8
TOK = 256
NS = 16
CH = 2048
EMB = 128
CW = 512
LANES = 128
BLK = 16
N_CTX = 64
LOG2E = 1.4426950408889634
SCALE2 = LOG2E / math.sqrt(HD)
VMEM = pl.BlockSpec(memory_space=pltpu.VMEM)
SMEM = pl.BlockSpec(memory_space=pltpu.SMEM)
AWAY = pl.BlockSpec(memory_space=pltpu.HBM)
F32 = jnp.float32
BF16 = jnp.bfloat16


def dot(a, b):
    return jnp.dot(a, b, preferred_element_type=F32)


def dot_t(a, b):
    return lax.dot_general(a, b, (((1,), (1,)), ((), ())), preferred_element_type=F32)


def pieces(x):
    hi = x.astype(BF16)
    rest = x - hi.astype(F32)
    mid = rest.astype(BF16)
    low = (rest - mid.astype(F32)).astype(BF16)
    return hi, mid, low


def softplus(v):
    return jnp.maximum(v, 0.0) + jnp.log1p(jnp.exp(-jnp.abs(v)))


def mixer_kernel(
    low_ref, proj_ref, bias_ref, chan_ref, log_ref, maps_ref,
    y_ref, cum_ref, send_ref, out_ref,
    step_s, flow_s, in_s,
):
    groups = CW // LANES

    @pl.when(pl.program_id(0) == 0)
    def _():
        in_map = maps_ref[0]
        for t in range(TOK):
            in_s[t] = jnp.broadcast_to(in_map[:, t : t + 1], (NS, LANES))
        spread = (
            lax.broadcasted_iota(jnp.int32, (NS, BLK * NS), 1) % NS
            == lax.broadcasted_iota(jnp.int32, (NS, BLK * NS), 0)
        ).astype(F32).astype(BF16)
        keep = (
            lax.broadcasted_iota(jnp.int32, (TOK, BLK * NS), 1) // NS
            == lax.broadcasted_iota(jnp.int32, (TOK, BLK * NS), 0) % BLK
        )
        hi, mid, _ = pieces(jnp.transpose(maps_ref[1]))
        for k, piece in enumerate((hi, mid)):
            rows = jnp.where(keep, dot(piece, spread), 0.0).astype(BF16)
            out_ref[:, k * BLK : (k + 1) * BLK, :] = rows.reshape(TOK // BLK, BLK, BLK * NS)

    rows = 64
    part = rows // BLK
    half = 2 * LANES
    shape = (rows, 2 * rows)
    triangle = (
        lax.broadcasted_iota(jnp.int32, shape, 0)
        >= lax.broadcasted_iota(jnp.int32, shape, 1) % rows
    ).astype(F32).astype(BF16)
    totals = []
    for c in range(CW // half):
        lanes = slice(c * half, (c + 1) * half)
        carry = jnp.zeros((1, half), F32)
        for r in range(TOK // rows):
            at = slice(r * rows, (r + 1) * rows)
            step = softplus(dot(low_ref[at, :], proj_ref[:, lanes]) + bias_ref[:, lanes])
            to = slice(r * part, (r + 1) * part)
            step_s[to, :, lanes] = step.reshape(part, BLK, half)
            flow = step * chan_ref[at, lanes].astype(F32)
            flow_s[to, :, lanes] = flow.reshape(part, BLK, half)
            hi, mid, _ = pieces(step)
            cum = dot(triangle, jnp.concatenate([hi, mid], 0)) + carry
            cum_ref[to, :, lanes] = cum.reshape(part, BLK, half)
            carry = cum[rows - 1 : rows, :]
        totals.append(carry)

    rate = -jnp.exp(log_ref[...]) * LOG2E
    rates = [rate[:, g * LANES : (g + 1) * LANES] for g in range(groups)]

    def block(j, states):
        states = list(states)
        past = []
        for t in range(BLK):
            gain = in_s[j * BLK + t]
            now = []
            for g in range(groups):
                lanes = slice(g * LANES, (g + 1) * LANES)
                decay = jnp.exp2(step_s[j, t : t + 1, lanes] * rates[g])
                states[g] = decay * states[g] + gain * flow_s[j, t : t + 1, lanes]
                now.append(states[g].astype(BF16))
            past.append(jnp.concatenate(now, 1))
        both = dot(out_ref[j], jnp.concatenate(past, 0))
        y_ref[j] = both[:BLK, :] + both[BLK:, :]
        return tuple(states)

    states = lax.fori_loop(
        0, TOK // BLK, block, tuple(jnp.zeros((NS, LANES), F32) for _ in range(groups)), unroll=2
    )
    total = jnp.concatenate(totals, 1)
    hi, mid, low = (v.astype(F32) for v in pieces(total))
    for g in range(groups):
        lanes = slice(g * LANES, (g + 1) * LANES)
        for k in range(NS // 4):
            send_ref[g * 4 + k] = jnp.concatenate(
                [
                    states[g][4 * k : 4 * k + 4, :], hi[:, lanes], mid[:, lanes], low[:, lanes],
                    jnp.zeros((1, LANES), F32),
                ],
                0,
            ).astype(BF16)


def run_mixer(step_low, step_proj, step_bias, channels, decay_log, state_maps):
    blocked = (TOK // BLK, BLK, CW)
    whole = jax.ShapeDtypeStruct((TOK // BLK, BLK, CH), F32)
    out_map = (TOK // BLK, 2 * BLK, BLK * NS)
    fixed = lambda shape: pl.BlockSpec(shape, lambda i: (0,) * len(shape))
    return pl.pallas_call(
        mixer_kernel,
        grid=(CH // CW,),
        in_specs=[
            fixed((TOK, 128)),
            pl.BlockSpec((128, CW), lambda i: (0, i)),
            pl.BlockSpec((1, CW), lambda i: (0, i)),
            pl.BlockSpec((TOK, CW), lambda i: (0, i)),
            pl.BlockSpec((NS, CW), lambda i: (0, i)),
            fixed((2, NS, TOK)),
        ],
        out_specs=[
            pl.BlockSpec(blocked, lambda i: (0, 0, i)),
            pl.BlockSpec(blocked, lambda i: (0, 0, i)),
            pl.BlockSpec((CW // LANES * 4, 8, LANES), lambda i: (i, 0, 0)),
            fixed(out_map),
        ],
        out_shape=[
            whole, whole, jax.ShapeDtypeStruct((N_CTX, 8, LANES), BF16),
            jax.ShapeDtypeStruct(out_map, BF16),
        ],
        scratch_shapes=[
            pltpu.VMEM(blocked, F32),
            pltpu.VMEM(blocked, F32),
            pltpu.VMEM((TOK, NS, LANES), F32),
        ],
        cost_estimate=pl.CostEstimate(
            flops=6_000_000_000, bytes_accessed=8 << 20, transcendentals=8 << 20
        ),
        name="mixer",
    )(step_low, step_proj, step_bias.reshape(1, CH), channels, decay_log, state_maps)


def prefix_kernel(pos_ref, got_ref, log_ref, out_ref):
    part = lax.rem(pos_ref[0], 4)
    rates = -jnp.exp(log_ref[...]) * LOG2E
    rate = rates[0:4]
    for k in range(1, 4):
        rate = jnp.where(part == k, rates[4 * k : 4 * k + 4], rate)
    state = jnp.zeros((4, LANES), F32)
    for s in range(N_CTX):
        out_ref[s] = state
        got = got_ref[s].astype(F32)
        total = got[4:5] + got[5:6] + got[6:7]
        state = jnp.exp2(rate * total) * state + got[0:4]


def run_prefix(position, got, decay_log):
    return pl.pallas_call(
        prefix_kernel,
        grid_spec=pltpu.PrefetchScalarGridSpec(
            num_scalar_prefetch=1,
            grid=(1,),
            in_specs=[
                pl.BlockSpec((N_CTX, 8, LANES), lambda i, pos: (0, 0, 0)),
                pl.BlockSpec((NS, LANES), lambda i, pos: (0, pos[0] // 4)),
            ],
            out_specs=pl.BlockSpec((N_CTX, 4, LANES), lambda i, pos: (0, 0, 0)),
        ),
        out_shape=jax.ShapeDtypeStruct((N_CTX, 4, LANES), F32),
        cost_estimate=pl.CostEstimate(flops=1 << 20, bytes_accessed=1 << 18, transcendentals=1 << 15),
        compiler_params=pltpu.CompilerParams(vmem_limit_bytes=8 << 20),
        name="prefix",
    )(position, got, decay_log)


def enter_kernel(
    y_ref, cum_ref, enter_ref, log_ref, out_ref, weight_ref, o_ref, total_s,
):
    groups = CW // LANES
    i = pl.program_id(0)
    rate = -jnp.exp(log_ref[...]) * LOG2E
    rates = [rate[:, g * LANES : (g + 1) * LANES] for g in range(groups)]
    enter = [
        jnp.concatenate([enter_ref[(i * groups + g) * 4 + k] for k in range(4)], 0)
        for g in range(groups)
    ]

    def block(j, carry):
        past = []
        for t in range(BLK):
            now = []
            for g in range(groups):
                lanes = slice(g * LANES, (g + 1) * LANES)
                decay = jnp.exp2(cum_ref[j, t : t + 1, lanes] * rates[g])
                now.append((decay * enter[g]).astype(BF16))
            past.append(jnp.concatenate(now, 1))
        both = dot(out_ref[j], jnp.concatenate(past, 0))
        rows = pl.ds(pl.multiple_of(j * BLK, BLK), BLK)
        total_s[i, rows, :] = y_ref[j] + both[:BLK, :] + both[BLK:, :]
        return carry

    lax.fori_loop(0, TOK // BLK, block, 0, unroll=2)

    @pl.when(i == CH // CW - 1)
    def _():
        square = jnp.zeros((TOK, LANES), F32)
        for k in range(CH // CW):
            for g in range(groups):
                piece = total_s[k, :, g * LANES : (g + 1) * LANES]
                square += piece * piece
        inverse = lax.rsqrt(jnp.sum(square, -1, keepdims=True) * (1.0 / CH) + 1e-05)
        mixed = jnp.zeros((TOK, EMB), F32)
        for k in range(CH // CW):
            mixed += dot((total_s[k] * inverse).astype(BF16), weight_ref[k * CW : (k + 1) * CW, :])
        o_ref[...] = mixed


def run_enter(y, cum, enter, decay_log, out_map, mixer_weight):
    blocked = pl.BlockSpec((TOK // BLK, BLK, CW), lambda i: (0, 0, i))
    fixed = lambda shape: pl.BlockSpec(shape, lambda i: (0,) * len(shape))
    return pl.pallas_call(
        enter_kernel,
        grid=(CH // CW,),
        in_specs=[
            blocked,
            blocked,
            VMEM,
            pl.BlockSpec((NS, CW), lambda i: (0, i)),
            fixed((TOK // BLK, 2 * BLK, BLK * NS)),
            fixed((CH, EMB)),
        ],
        out_specs=fixed((TOK, EMB)),
        out_shape=jax.ShapeDtypeStruct((TOK, EMB), F32),
        scratch_shapes=[pltpu.VMEM((CH // CW, TOK, CW), F32)],
        cost_estimate=pl.CostEstimate(
            flops=4_000_000_000, bytes_accessed=6 << 20, transcendentals=8 << 20
        ),
        name="enter",
    )(y, cum, enter, decay_log, out_map, mixer_weight)


def final_kernel(mixed_ref, own_ref, back_ref, o_ref):
    combined = mixed_ref[...] + jnp.transpose(own_ref[...] + back_ref[...].astype(F32))
    mean = jnp.mean(combined * combined, -1, keepdims=True)
    o_ref[...] = (combined * lax.rsqrt(mean + 1e-06)).astype(BF16)


def run_final(mixed, own, back):
    return pl.pallas_call(
        final_kernel,
        in_specs=[pl.BlockSpec(memory_space=pltpu.VMEM)] * 3,
        out_specs=pl.BlockSpec(memory_space=pltpu.VMEM),
        out_shape=jax.ShapeDtypeStruct((TOK, EMB), BF16),
        cost_estimate=pl.CostEstimate(flops=1 << 18, bytes_accessed=1 << 18, transcendentals=256),
        compiler_params=pltpu.CompilerParams(vmem_limit_bytes=8 << 20),
        name="final",
    )(mixed, own, back)


def scores_kernel(pos_ref, q_ref, p_ref, k0_ref, k1_ref, k2_ref, away_ref, stat_ref, raw, w_ref, sems):
    def out(h):
        return pltpu.make_async_copy(w_ref.at[h], away_ref.at[h], sems.at[h])

    def head(h, carry):
        scores_head(h, pos_ref, q_ref, p_ref, k0_ref, k1_ref, k2_ref, w_ref, stat_ref, raw)
        out(h).start()
        return carry

    lax.fori_loop(0, HEADS, head, 0)
    for h in range(HEADS):
        out(h).wait()


def scores_head(h, pos_ref, q_ref, p_ref, k0_ref, k1_ref, k2_ref, w_ref, stat_ref, raw):
    span = pl.ds(pl.multiple_of(h * HD, HD), HD)
    side = lax.rem(pos_ref[0], 2)
    pair = pos_ref[0] // 2
    gone1 = jnp.where(pair >= 1, 0.0, -1e30).astype(F32)
    gone2 = jnp.where(pair >= 2, 0.0, -1e30).astype(F32)
    key = lax.broadcasted_iota(jnp.int32, (HD, HD), 0)
    asker = lax.broadcasted_iota(jnp.int32, (HD, HD), 1)
    line = lax.broadcasted_iota(jnp.int32, (4 * HEADS, TOK), 0)
    k0, k1, k2 = k0_ref[:, span], k1_ref[:, span], k2_ref[:, span]
    zero = jnp.zeros((HD, HD), BF16)

    def weigh(first, kinds, gone, slot):
        tops, sums = [], []
        for side_q in range(2):
            lanes = slice(side_q * HD, (side_q + 1) * HD)

            def load(n, side_k):
                at = (first + n) * TOK + side_k * HD
                x = raw[at : at + HD, lanes]
                kind = kinds[n][side_k][side_q]
                if kind == "upto":
                    x = jnp.where(key <= asker, x, -1e30)
                if kind == "after":
                    x = jnp.where(key > asker, x, -1e30)
                return x

            top = None
            for n in range(len(kinds)):
                block = None
                for side_k in range(2):
                    if kinds[n][side_k][side_q] != "none":
                        x = jnp.max(load(n, side_k), 0, keepdims=True)
                        block = x if block is None else jnp.maximum(block, x)
                block = block * SCALE2 + gone[n]
                top = block if top is None else jnp.maximum(top, block)
            total = jnp.zeros((1, HD), F32)
            for n in range(len(kinds)):
                level = top - gone[n]
                for side_k in range(2):
                    at = (first + n) * TOK + side_k * HD
                    if kinds[n][side_k][side_q] == "none":
                        w_ref[h, at : at + HD, lanes] = zero
                        continue
                    terms = jnp.exp2(load(n, side_k) * SCALE2 - level)
                    total += jnp.sum(terms, 0, keepdims=True)
                    w_ref[h, at : at + HD, lanes] = terms.astype(BF16)
            tops.append(top)
            sums.append(total)
        now = jnp.where(line == slot + h, jnp.concatenate(tops, 1), stat_ref[...])
        stat_ref[...] = jnp.where(line == slot + HEADS + h, jnp.concatenate(sums, 1), now)

    q, other = q_ref[:, span], p_ref[:, span]
    for n, k in enumerate((k0, k1, k2)):
        raw[n * TOK : (n + 1) * TOK, :] = dot_t(k, q)
    raw[3 * TOK : 4 * TOK, :] = dot_t(jnp.where(side == 0, k0, k1), other)
    raw[4 * TOK : 5 * TOK, :] = dot_t(jnp.where(side == 0, k1, k2), other)
    every = (("all", "all"), ("all", "all"))
    weigh(
        0,
        ((("upto", "all"), ("none", "upto")), every, (("after", "none"), ("all", "after"))),
        (jnp.float32(0.0), gone1, gone2),
        0,
    )
    weigh(
        3,
        (every, every),
        (jnp.where(side == 0, 0.0, gone1), jnp.where(side == 0, gone1, gone2)),
        2 * HEADS,
    )


def run_scores(position, query, other, k0, k1, k2):
    return pl.pallas_call(
        scores_kernel,
        in_specs=[SMEM] + [VMEM] * 5,
        out_specs=[AWAY, VMEM],
        scratch_shapes=[
            pltpu.VMEM((5 * TOK, TOK), F32),
            pltpu.VMEM((HEADS, 5 * TOK, TOK), BF16),
            pltpu.SemaphoreType.DMA((HEADS,)),
        ],
        out_shape=[
            pltpu.HBM((HEADS, 5 * TOK, TOK), BF16),
            jax.ShapeDtypeStruct((4 * HEADS, TOK), F32),
        ],
        compiler_params=pltpu.CompilerParams(vmem_limit_bytes=16 << 20),
        cost_estimate=pl.CostEstimate(
            flops=700_000_000, bytes_accessed=8 << 20, transcendentals=3 << 20
        ),
        name="scores",
    )(position, query, other, k0, k1, k2)


def dot_0(a, b):
    return lax.dot_general(a, b, (((0,), (0,)), ((), ())), preferred_element_type=F32)


def values_kernel(
    mine, pos_ref, away_ref, v0_ref, v1_ref, v2_ref, stat_ref, got_ref, weight_ref, o_ref,
    scale_s, sum_s, w_ref, sems,
):
    rows = (0, 3 * TOK) if mine else (3 * TOK, 2 * TOK)

    def fetch(h):
        return pltpu.make_async_copy(away_ref.at[h, pl.ds(*rows), :], w_ref.at[h], sems.at[h])

    for h in range(HEADS):
        fetch(h).start()
    side = lax.rem(pos_ref[0], 2)
    at = lambda ref, k: (ref[k * 8 : k * 8 + 8, :], ref[k * 8 + 8 : k * 8 + 16, :])
    (m0, l0), (m1, l1) = at(stat_ref, 0 if mine else 2), at(got_ref, 2 if mine else 0)
    top = jnp.maximum(m0, m1)
    f0 = jnp.exp2(m0 - top)
    scale_s[...] = f0 / (l0 * f0 + l1 * jnp.exp2(m1 - top))
    sum_s[...] = jnp.zeros_like(sum_s)
    line = lax.broadcasted_iota(jnp.int32, (HEADS, TOK), 0)

    def head(h, carry):
        span = pl.ds(pl.multiple_of(h * HD, HD), HD)
        scale = jnp.sum(jnp.where(line == h, scale_s[...], 0.0), 0, keepdims=True)
        v0, v1, v2 = v0_ref[:, span], v1_ref[:, span], v2_ref[:, span]
        fetch(h).wait()
        w = lambda n: w_ref[h, n * TOK : (n + 1) * TOK, :]
        if mine:
            taken = dot_0(v0, w(0)) + dot_0(v1, w(1)) + dot_0(v2, w(2))
        else:
            taken = dot_0(jnp.where(side == 0, v0, v1), w(0))
            taken += dot_0(jnp.where(side == 0, v1, v2), w(1))
        sum_s[...] += dot_0(weight_ref[span, :], (taken * scale).astype(BF16))
        return carry

    lax.fori_loop(0, HEADS, head, 0, unroll=2)
    o_ref[...] = sum_s[...].astype(o_ref.dtype)


def run_values(mine, position, weights, v0, v1, v2, stats, got, attend_weight):
    return pl.pallas_call(
        functools.partial(values_kernel, mine),
        in_specs=[SMEM, AWAY] + [VMEM] * 6,
        out_specs=VMEM,
        scratch_shapes=[
            pltpu.VMEM((HEADS, TOK), F32),
            pltpu.VMEM((EMB, TOK), F32),
            pltpu.VMEM((HEADS, (3 if mine else 2) * TOK, TOK), BF16),
            pltpu.SemaphoreType.DMA((HEADS,)),
        ],
        out_shape=jax.ShapeDtypeStruct((EMB, TOK), F32 if mine else BF16),
        compiler_params=pltpu.CompilerParams(vmem_limit_bytes=16 << 20),
        cost_estimate=pl.CostEstimate(
            flops=400_000_000, bytes_accessed=4 << 20, transcendentals=1 << 12
        ),
        name="values_own" if mine else "values_other",
    )(position, weights, v0, v1, v2, stats, got, attend_weight)


def shift(value, steps):
    return lax.ppermute(value, "ctx", [(s, s + steps) for s in range(N_CTX - steps)])


def swap(value):
    return lax.ppermute(value, "ctx", [(s, s ^ 1) for s in range(N_CTX)])


def per_device(
    query_rows, key_rows, value_rows, channels, step_low, step_proj, step_bias, decay_log,
    state_maps, attend_weight, mixer_weight,
):
    position = lax.axis_index("ctx").astype(jnp.int32).reshape(1)
    other = swap(query_rows)
    k1 = shift(key_rows, 2)
    k2 = shift(key_rows, 4)
    y, cum, send, out_map = run_mixer(
        step_low, step_proj, step_bias, channels, decay_log, state_maps
    )
    got = lax.all_to_all(send, "ctx", 0, 0, tiled=True)
    v1 = shift(value_rows, 2)
    v2 = shift(value_rows, 4)
    weights, stats = run_scores(position, query_rows, other, key_rows, k1, k2)
    given = run_prefix(position, got, decay_log)
    enter = lax.all_to_all(given, "ctx", 0, 0, tiled=True)
    got_stats = swap(stats)
    blocks = (value_rows, v1, v2, stats, got_stats, attend_weight)
    weights = pltpu.with_memory_space_constraint(weights, pltpu.HBM)
    give = run_values(False, position, weights, *blocks)
    back = swap(give)
    mixed = run_enter(y, cum, enter, decay_log, out_map, mixer_weight)
    own = run_values(True, position, weights, *blocks)
    return run_final(mixed, own, back)


def solution(mesh):
    rows = P(("dp", "ctx"), None)
    return jax.shard_map(
        per_device,
        mesh=mesh,
        in_specs=(rows, rows, rows, rows, rows, P(), P(), P(), P(None, None, ("dp", "ctx")), P(), P()),
        out_specs=rows,
        check_vma=False,
    )
```

time: 149 us -> 132 us (0.89)
  Pallas kernels: 64.7 us -> 45.9 us
  waiting for transfers between devices: 21.6 us -> 28.2 us
  local copies, waits for them, and re-layouts: 3.67 us -> 0.68 us
    pallas_call x1, Pallas kernels: 26.3 us -> 16.4 us  [run_mixer(): pl.pallas_call(mixer_kernel, grid=(CH // CW,), in_specs=[fixed((TOK, 128)...]
    all_to_all x1, waiting for transfers between devices: 16.1 us -> 25.7 us  [per_device(): got = lax.all_to_all(send, 'ctx', 0, 0, tiled=True)]
    pallas_call x3 -> x5, Pallas kernels: 36.7 us -> 28.7 us  [the longest x1 11.8 us: run_enter(): pl.pallas_call(enter_kernel, grid=(CH // CW,), in_specs=[blocked, blocked...]
    ppermute x3, waiting for transfers between devices: 5.51 us -> 2.51 us  [swap(): return lax.ppermute(value, 'ctx', [(s, s ^ 1) for s in range(N_CTX)])]
    unnamed x18 -> x14, local copies, waits for them, and re-layouts: 3.67 us -> 0.68 us
  transfers between devices with their start and end apart: 9 -> 9, of which waited for: 3 -> 2; matrix products, arithmetic and copies ran while one was open for 1% -> 0% of each run, Pallas kernels for 31% -> 34%
where the time goes in v2:
time: 132 us
  starting transfers between devices  56.8 us (43%)
  Pallas kernels  45.9 us (35%)
  waiting for transfers between devices  28.2 us (21%)
    all_to_all x1, waiting for transfers between devices, per_device(): got = lax.all_to_all(send, 'ctx', 0, 0, tiled=True)  25.7 us
    ppermute x3, starting transfers between devices, swap(): return lax.ppermute(value, 'ctx', [(s, s ^ 1) for s in range(N_CTX)])  25.5 us
    pallas_call x1, Pallas kernels, run_mixer(): pl.pallas_call(mixer_kernel, grid=(CH // CW,), in_specs=[fixed((TOK, 128)...  16.4 us
    ppermute x4, starting transfers between devices, shift(): lax.ppermute(value, 'ctx', [(s, s + steps) for s in range(N_CTX - steps)])  15.5 us
    pallas_call x1, Pallas kernels, run_enter(): pl.pallas_call(enter_kernel, grid=(CH // CW,), in_specs=[blocked, blocked...  11.8 us
    pallas_call x2, Pallas kernels, run_values(): pl.pallas_call(functools.partial(values_kernel, mine), in_specs=[SMEM, AW...  9.26 us
    all_to_all x1, starting transfers between devices, per_device(): got = lax.all_to_all(send, 'ctx', 0, 0, tiled=True)  8.19 us
    all_to_all x1, starting transfers between devices, per_device(): enter = lax.all_to_all(given, 'ctx', 0, 0, tiled=True)  7.62 us
  transfers between devices with their start and end apart: 9, of which 2 were waited for; matrix products, arithmetic and copies ran while one was open for 0% of the time, Pallas kernels for 34%

profile of v2, /device:TPU:2, one launch (start us, length us, event | category | flops | bytes accessed | tf_op | source)
XLA Modules:
  0.0 131.8 jit_solution(14523073311756216318)
XLA Ops:
  0.0 3.4 %collective-permute-start.1 = (bf16[256,1024]{1,0:T(8,128)(2,1)}, bf16[256,1024]{1,0:T(8,128)(2,1)}, u32[]{:S(2)}, u32[]{:S(2)}) collective-permute-start(bf16[256,1024]{1,0:T(8,128)(2,1)} %k0_ref.1), channel_id=1, source_target_pairs={{0,16},{8,24},{16,32},{24,40},{32,48},{40,56},{48,64},{56,72},{64,... | collective-permute-start | bytes 1572872 | tf_op jit(solution)/shard_map/ppermute | solution.py:463
  3.4 4.8 %collective-permute-start.2 = (bf16[256,1024]{1,0:T(8,128)(2,1)}, bf16[256,1024]{1,0:T(8,128)(2,1)}, u32[]{:S(2)}, u32[]{:S(2)}) collective-permute-start(bf16[256,1024]{1,0:T(8,128)(2,1)} %k0_ref.1), channel_id=1, source_target_pairs={{0,32},{8,40},{16,48},{24,56},{32,64},{40,72},{48,80},{56,88},{64,... | collective-permute-start | bytes 1572872 | tf_op jit(solution)/shard_map/ppermute | solution.py:463
  8.2 2.0 %collective-permute-start.3 = (bf16[256,1024]{1,0:T(8,128)(2,1)}, bf16[256,1024]{1,0:T(8,128)(2,1)S(1)}, u32[]{:S(2)}, u32[]{:S(2)}) collective-permute-start(bf16[256,1024]{1,0:T(8,128)(2,1)} %v0_ref.3), channel_id=1, source_target_pairs={{0,16},{8,24},{16,32},{24,40},{32,48},{40,56},{48,64},{56,72},{64,... | collective-permute-start | bytes 1572872 | tf_op jit(solution)/shard_map/ppermute | solution.py:463
  10.2 5.3 %collective-permute-start.4 = (bf16[256,1024]{1,0:T(8,128)(2,1)}, bf16[256,1024]{1,0:T(8,128)(2,1)S(1)}, u32[]{:S(2)}, u32[]{:S(2)}) collective-permute-start(bf16[256,1024]{1,0:T(8,128)(2,1)} %v0_ref.3), channel_id=1, source_target_pairs={{0,32},{8,40},{16,48},{24,56},{32,64},{40,72},{48,80},{56,88},{64,... | collective-permute-start | bytes 1572872 | tf_op jit(solution)/shard_map/ppermute | solution.py:463
  15.5 10.9 %collective-permute-start = (bf16[256,1024]{1,0:T(8,128)(2,1)}, bf16[256,1024]{1,0:T(8,128)(2,1)}, u32[]{:S(2)}, u32[]{:S(2)}) collective-permute-start(bf16[256,1024]{1,0:T(8,128)(2,1)} %q_ref.1), channel_id=1, source_target_pairs={{0,8},{8,0},{16,24},{24,16},{32,40},{40,32},{48,56},{56,48},{64,72... | collective-permute-start | bytes 1572872 | tf_op jit(solution)/shard_map/ppermute | solution.py:467
  26.5 0.0 copy-start.3
  26.5 16.4 %mixer.1 = (f32[16,16,2048]{2,1,0:T(8,128)}, f32[16,16,2048]{2,1,0:T(8,128)}, bf16[64,8,128]{2,1,0:T(8,128)(2,1)}, bf16[16,32,256]{2,1,0:T(8,128)(2,1)}) custom-call(bf16[256,128]{1,0:T(8,128)(2,1)} %low_ref.1, bf16[128,2048]{1,0:T(8,128)(2,1)} %proj_ref.1, f32[1,2048]{1,0:T(1,128)} %bitcast.2, bf16[256,2048]{1,0:T(8,128)(2,1)} %chan_ref.1, ...), custom_call_target="tpu_custom_call" | custom-call | flops 6000000000 | bytes 8388608 | tf_op jit(solution)/shard_map/mixer/pallas_call | solution.py:142
  42.9 8.2 %all-to-all-start = ((bf16[64,8,128]{2,1,0:T(8,128)(2,1)}), bf16[64,8,128]{2,1,0:T(8,128)(2,1)S(1)}, u32[]{:S(2)}, u32[]{:S(2)}) async-start(bf16[64,8,128]{2,1,0:T(8,128)(2,1)} %get-tuple-element.13), calls=%async_computation | async-start | bytes 262144 | tf_op jit(solution)/shard_map/all_to_all | solution.py:481
  51.1 25.7 %all-to-all-done.got_ref = bf16[64,8,128]{2,1,0:T(8,128)(2,1)S(1)} async-done(((bf16[64,8,128]{2,1,0:T(8,128)(2,1)}), bf16[64,8,128]{2,1,0:T(8,128)(2,1)S(1)}, u32[]{:S(2)}, u32[]{:S(2)}) %all-to-all-start) | async-done | bytes 131104 | tf_op jit(solution)/shard_map/all_to_all | solution.py:481
  76.7 0.8 prefix.1
  77.5 7.6 %all-to-all-start.1 = ((f32[64,4,128]{2,1,0:T(4,128)}), f32[64,4,128]{2,1,0:T(4,128)S(1)}, u32[]{:S(2)}, u32[]{:S(2)}) async-start(f32[64,4,128]{2,1,0:T(4,128)} %prefix.1), calls=%async_computation.1 | async-start | bytes 262144 | tf_op jit(solution)/shard_map/all_to_all | solution.py:486
  85.2 0.0 copy-start
  85.2 0.0 copy-start.1
  85.2 0.0 collective-permute-done.p_ref
  85.2 0.0 collective-permute-done.1.k1_ref
  85.2 0.0 collective-permute-done.2.k2_ref
  85.2 0.0 copy-done.4
  85.2 0.0 copy-done.5
  85.2 6.8 %scores.1 = (bf16[8,1280,256]{2,1,0:T(8,128)(2,1)}, f32[32,256]{1,0:T(8,128)S(1)}) custom-call(s32[1]{0:T(128)} %bitcast.1.pos_ref, bf16[256,1024]{1,0:T(8,128)(2,1)S(1)} %copy-done.4, bf16[256,1024]{1,0:T(8,128)(2,1)} %collective-permute-done.p_ref, bf16[256,1024]{1,0:T(8,128)(2,1)S(1)} %copy-done.5, bf16[256,1024]{1,0:T(8,128)(2,1)} %collective-permute-done.1.k1_ref, ...), custom_call_target="tpu_custom_call" | custom-call | flops 700000000 | bytes 8388608 | tf_op jit(solution)/shard_map/scores/pallas_call | solution.py:379
  92.1 7.3 %collective-permute-start.5 = (f32[32,256]{1,0:T(8,128)S(1)}, f32[32,256]{1,0:T(8,128)S(1)}, u32[]{:S(2)}, u32[]{:S(2)}) collective-permute-start(f32[32,256]{1,0:T(8,128)S(1)} %get-tuple-element.16.stat_ref), channel_id=1, source_target_pairs={{0,8},{8,0},{16,24},{24,16},{32,40},{40,32},{48,56},{56,48},{64,72... | collective-permute-start | bytes 98312 | tf_op jit(solution)/shard_map/ppermute | solution.py:467
  99.4 0.0 collective-permute-done.3.v1_ref
  99.4 0.0 collective-permute-done.4.v2_ref
  99.4 2.5 %collective-permute-done.5.got_ref = f32[32,256]{1,0:T(8,128)S(1)} collective-permute-done((f32[32,256]{1,0:T(8,128)S(1)}, f32[32,256]{1,0:T(8,128)S(1)}, u32[]{:S(2)}, u32[]{:S(2)}) %collective-permute-start.5) | collective-permute-done | bytes 32800 | tf_op jit(solution)/shard_map/ppermute | solution.py:467
  101.9 4.5 %values_other.1 = bf16[128,256]{1,0:T(8,128)(2,1)S(1)} custom-call(s32[1]{0:T(128)} %bitcast.1.pos_ref, bf16[8,1280,256]{2,1,0:T(8,128)(2,1)} %get-tuple-element.15.away_ref, bf16[256,1024]{1,0:T(8,128)(2,1)S(1)} %copy-done, bf16[256,1024]{1,0:T(8,128)(2,1)S(1)} %collective-permute-done.3.v1_ref, bf16[256,1024]{1,0:T(8,128)(2,1)S(1)} %collective-permute-done.4.v2_ref, ...), custom_call_target="tpu_custom_call" | custom-call | flops 400000000 | bytes 4194304 | tf_op jit(solution)/shard_map/values_other/pallas_call | solution.py:443
  106.4 7.3 %collective-permute-start.6 = (bf16[128,256]{1,0:T(8,128)(2,1)S(1)}, bf16[128,256]{1,0:T(8,128)(2,1)S(1)}, u32[]{:S(2)}, u32[]{:S(2)}) collective-permute-start(bf16[128,256]{1,0:T(8,128)(2,1)S(1)} %values_other.1), channel_id=1, source_target_pairs={{0,8},{8,0},{16,24},{24,16},{32,40},{40,32},{48,56},{56,48},{64,72... | collective-permute-start | bytes 196616 | tf_op jit(solution)/shard_map/ppermute | solution.py:467
  113.7 0.0 all-to-all-done.1.enter_ref
  113.7 0.0 copy-start.6
  113.7 0.6 copy-done.6
  114.3 11.8 %enter.1.mixed_ref = f32[256,128]{1,0:T(8,128)} custom-call(f32[16,16,2048]{2,1,0:T(8,128)} %get-tuple-element.11.y_ref, f32[16,16,2048]{2,1,0:T(8,128)} %get-tuple-element.12.cum_ref, f32[64,4,128]{2,1,0:T(4,128)} %copy-done.6, f32[16,2048]{1,0:T(8,128)} %log_ref.5, bf16[16,32,256]{2,1,0:T(8,128)(2,1)} %get-tuple-element.14.out_ref, ...), custom_call_target="tpu_custom_call" | custom-call | flops 4000000000 | bytes 6291456 | tf_op jit(solution)/shard_map/enter/pallas_call | solution.py:253
  126.1 4.8 %values_own.1.own_ref = f32[128,256]{1,0:T(8,128)S(1)} custom-call(s32[1]{0:T(128)} %bitcast.1.pos_ref, bf16[8,1280,256]{2,1,0:T(8,128)(2,1)} %get-tuple-element.15.away_ref, bf16[256,1024]{1,0:T(8,128)(2,1)S(1)} %copy-done, bf16[256,1024]{1,0:T(8,128)(2,1)S(1)} %collective-permute-done.3.v1_ref, bf16[256,1024]{1,0:T(8,128)(2,1)S(1)} %collective-permute-done.4.v2_ref, ...), custom_call_target="tpu_custom_call" | custom-call | flops 400000000 | bytes 4194304 | tf_op jit(solution)/shard_map/values_own/pallas_call | solution.py:443
  130.9 0.0 collective-permute-done.6.back_ref
  130.9 0.8 final.1
  (7 shorter events, 0.0 us)
Async XLA Ops:
  0.0 85.2 %collective-permute-start.1 = (bf16[256,1024]{1,0:T(8,128)(2,1)}, bf16[256,1024]{1,0:T(8,128)(2,1)}, u32[]{:S(2)}, u32[]{:S(2)}) collective-permute-start(bf16[256,1024]{1,0:T(8,128)(2,1)} %k0_ref.1), channel_id=1, source_target_pairs={{0,16},{8,24},{16,32},{24,40},{32,48},{40,56},{48,64},{56,72},{64,... | collective-permute-start | bytes 1572872 | tf_op jit(solution)/shard_map/ppermute | solution.py:463
  3.4 81.8 %collective-permute-start.2 = (bf16[256,1024]{1,0:T(8,128)(2,1)}, bf16[256,1024]{1,0:T(8,128)(2,1)}, u32[]{:S(2)}, u32[]{:S(2)}) collective-permute-start(bf16[256,1024]{1,0:T(8,128)(2,1)} %k0_ref.1), channel_id=1, source_target_pairs={{0,32},{8,40},{16,48},{24,56},{32,64},{40,72},{48,80},{56,88},{64,... | collective-permute-start | bytes 1572872 | tf_op jit(solution)/shard_map/ppermute | solution.py:463
  8.2 91.2 %collective-permute-start.3 = (bf16[256,1024]{1,0:T(8,128)(2,1)}, bf16[256,1024]{1,0:T(8,128)(2,1)S(1)}, u32[]{:S(2)}, u32[]{:S(2)}) collective-permute-start(bf16[256,1024]{1,0:T(8,128)(2,1)} %v0_ref.3), channel_id=1, source_target_pairs={{0,16},{8,24},{16,32},{24,40},{32,48},{40,56},{48,64},{56,72},{64,... | collective-permute-start | bytes 1572872 | tf_op jit(solution)/shard_map/ppermute | solution.py:463
  10.2 89.1 %collective-permute-start.4 = (bf16[256,1024]{1,0:T(8,128)(2,1)}, bf16[256,1024]{1,0:T(8,128)(2,1)S(1)}, u32[]{:S(2)}, u32[]{:S(2)}) collective-permute-start(bf16[256,1024]{1,0:T(8,128)(2,1)} %v0_ref.3), channel_id=1, source_target_pairs={{0,32},{8,40},{16,48},{24,56},{32,64},{40,72},{48,80},{56,88},{64,... | collective-permute-start | bytes 1572872 | tf_op jit(solution)/shard_map/ppermute | solution.py:463
  15.5 69.7 %collective-permute-start = (bf16[256,1024]{1,0:T(8,128)(2,1)}, bf16[256,1024]{1,0:T(8,128)(2,1)}, u32[]{:S(2)}, u32[]{:S(2)}) collective-permute-start(bf16[256,1024]{1,0:T(8,128)(2,1)} %q_ref.1), channel_id=1, source_target_pairs={{0,8},{8,0},{16,24},{24,16},{32,40},{40,32},{48,56},{56,48},{64,72... | collective-permute-start | bytes 1572872 | tf_op jit(solution)/shard_map/ppermute | solution.py:467
  26.5 50.3 %copy-start.3 = (f32[16,2048]{1,0:T(8,128)S(1)}, f32[16,2048]{1,0:T(8,128)}, u32[]{:S(2)}) copy-start(f32[16,2048]{1,0:T(8,128)} %log_ref.5) | copy-start | bytes 393220
  26.5 58.8 %copy-start.4 = (bf16[256,1024]{1,0:T(8,128)(2,1)S(1)}, bf16[256,1024]{1,0:T(8,128)(2,1)}, u32[]{:S(2)}) copy-start(bf16[256,1024]{1,0:T(8,128)(2,1)} %q_ref.1) | copy-start | bytes 1572868
  26.5 58.8 %copy-start.5 = (bf16[256,1024]{1,0:T(8,128)(2,1)S(1)}, bf16[256,1024]{1,0:T(8,128)(2,1)}, u32[]{:S(2)}) copy-start(bf16[256,1024]{1,0:T(8,128)(2,1)} %k0_ref.1) | copy-start | bytes 1572868
  42.9 33.9 %all-to-all-start = ((bf16[64,8,128]{2,1,0:T(8,128)(2,1)}), bf16[64,8,128]{2,1,0:T(8,128)(2,1)S(1)}, u32[]{:S(2)}, u32[]{:S(2)}) async-start(bf16[64,8,128]{2,1,0:T(8,128)(2,1)} %get-tuple-element.13), calls=%async_computation | async-start | bytes 262144 | tf_op jit(solution)/shard_map/all_to_all | solution.py:481
  77.5 36.1 %all-to-all-start.1 = ((f32[64,4,128]{2,1,0:T(4,128)}), f32[64,4,128]{2,1,0:T(4,128)S(1)}, u32[]{:S(2)}, u32[]{:S(2)}) async-start(f32[64,4,128]{2,1,0:T(4,128)} %prefix.1), calls=%async_computation.1 | async-start | bytes 262144 | tf_op jit(solution)/shard_map/all_to_all | solution.py:486
  85.2 16.7 %copy-start = (bf16[256,1024]{1,0:T(8,128)(2,1)S(1)}, bf16[256,1024]{1,0:T(8,128)(2,1)}, u32[]{:S(2)}) copy-start(bf16[256,1024]{1,0:T(8,128)(2,1)} %v0_ref.3) | copy-start | bytes 1572868
  85.2 16.7 %copy-start.1 = (bf16[1024,128]{1,0:T(8,128)(2,1)S(1)}, bf16[1024,128]{1,0:T(8,128)(2,1)}, u32[]{:S(2)}) copy-start(bf16[1024,128]{1,0:T(8,128)(2,1)} %weight_ref.5) | copy-start | bytes 786436
  92.1 9.8 %collective-permute-start.5 = (f32[32,256]{1,0:T(8,128)S(1)}, f32[32,256]{1,0:T(8,128)S(1)}, u32[]{:S(2)}, u32[]{:S(2)}) collective-permute-start(f32[32,256]{1,0:T(8,128)S(1)} %get-tuple-element.16.stat_ref), channel_id=1, source_target_pairs={{0,8},{8,0},{16,24},{24,16},{32,40},{40,32},{48,56},{56,48},{64,72... | collective-permute-start | bytes 98312 | tf_op jit(solution)/shard_map/ppermute | solution.py:467
  106.4 24.5 %collective-permute-start.6 = (bf16[128,256]{1,0:T(8,128)(2,1)S(1)}, bf16[128,256]{1,0:T(8,128)(2,1)S(1)}, u32[]{:S(2)}, u32[]{:S(2)}) collective-permute-start(bf16[128,256]{1,0:T(8,128)(2,1)S(1)} %values_other.1), channel_id=1, source_target_pairs={{0,8},{8,0},{16,24},{24,16},{32,40},{40,32},{48,56},{56,48},{64,72... | collective-permute-start | bytes 196616 | tf_op jit(solution)/shard_map/ppermute | solution.py:467
  113.7 0.7 copy-start.6
  126.1 4.8 %copy-start.2 = (f32[256,128]{1,0:T(8,128)S(1)}, f32[256,128]{1,0:T(8,128)}, u32[]{:S(2)}) copy-start(f32[256,128]{1,0:T(8,128)} %enter.1.mixed_ref) | copy-start | bytes 393220

commit v3 on v2

--- a/solution.py
+++ b/solution.py
@@ -118,7 +118,7 @@
         return tuple(states)
 
     states = lax.fori_loop(
-        0, TOK // BLK, block, tuple(jnp.zeros((NS, LANES), F32) for _ in range(groups)), unroll=2
+        0, TOK // BLK, block, tuple(jnp.zeros((NS, LANES), F32) for _ in range(groups)), unroll=4
     )
     total = jnp.concatenate(totals, 1)
     hi, mid, low = (v.astype(F32) for v in pieces(total))
@@ -206,7 +206,7 @@
 
 
 def enter_kernel(
-    y_ref, cum_ref, enter_ref, log_ref, out_ref, weight_ref, o_ref, total_s,
+    y_ref, cum_ref, enter_ref, log_ref, out_ref, weight_ref, own_ref, back_ref, o_ref, total_s,
 ):
     groups = CW // LANES
     i = pl.program_id(0)
@@ -231,7 +231,7 @@
         total_s[i, rows, :] = y_ref[j] + both[:BLK, :] + both[BLK:, :]
         return carry
 
-    lax.fori_loop(0, TOK // BLK, block, 0, unroll=2)
+    lax.fori_loop(0, TOK // BLK, block, 0, unroll=4)
 
     @pl.when(i == CH // CW - 1)
     def _():
@@ -241,14 +241,16 @@
                 piece = total_s[k, :, g * LANES : (g + 1) * LANES]
                 square += piece * piece
         inverse = lax.rsqrt(jnp.sum(square, -1, keepdims=True) * (1.0 / CH) + 1e-05)
-        mixed = jnp.zeros((TOK, EMB), F32)
+        combined = jnp.transpose(own_ref[...] + back_ref[...].astype(F32))
         for k in range(CH // CW):
-            mixed += dot((total_s[k] * inverse).astype(BF16), weight_ref[k * CW : (k + 1) * CW, :])
-        o_ref[...] = mixed
-
-
-def run_enter(y, cum, enter, decay_log, out_map, mixer_weight):
+            combined += dot((total_s[k] * inverse).astype(BF16), weight_ref[k * CW : (k + 1) * CW, :])
+        mean = jnp.mean(combined * combined, -1, keepdims=True)
+        o_ref[...] = (combined * lax.rsqrt(mean + 1e-06)).astype(BF16)
+
+
+def run_enter(y, cum, enter, decay_log, out_map, mixer_weight, own, back):
     blocked = pl.BlockSpec((TOK // BLK, BLK, CW), lambda i: (0, 0, i))
+    far = lambda x: pltpu.with_memory_space_constraint(x, pltpu.HBM)
     fixed = lambda shape: pl.BlockSpec(shape, lambda i: (0,) * len(shape))
     return pl.pallas_call(
         enter_kernel,
@@ -260,33 +262,18 @@
             pl.BlockSpec((NS, CW), lambda i: (0, i)),
             fixed((TOK // BLK, 2 * BLK, BLK * NS)),
             fixed((CH, EMB)),
+            VMEM,
+            VMEM,
         ],
         out_specs=fixed((TOK, EMB)),
-        out_shape=jax.ShapeDtypeStruct((TOK, EMB), F32),
+        out_shape=jax.ShapeDtypeStruct((TOK, EMB), BF16),
         scratch_shapes=[pltpu.VMEM((CH // CW, TOK, CW), F32)],
         cost_estimate=pl.CostEstimate(
             flops=4_000_000_000, bytes_accessed=6 << 20, transcendentals=8 << 20
         ),
+        compiler_params=pltpu.CompilerParams(vmem_limit_bytes=20 << 20),
         name="enter",
-    )(y, cum, enter, decay_log, out_map, mixer_weight)
-
-
-def final_kernel(mixed_ref, own_ref, back_ref, o_ref):
-    combined = mixed_ref[...] + jnp.transpose(own_ref[...] + back_ref[...].astype(F32))
-    mean = jnp.mean(combined * combined, -1, keepdims=True)
-    o_ref[...] = (combined * lax.rsqrt(mean + 1e-06)).astype(BF16)
-
-
-def run_final(mixed, own, back):
-    return pl.pallas_call(
-        final_kernel,
-        in_specs=[pl.BlockSpec(memory_space=pltpu.VMEM)] * 3,
-        out_specs=pl.BlockSpec(memory_space=pltpu.VMEM),
-        out_shape=jax.ShapeDtypeStruct((TOK, EMB), BF16),
-        cost_estimate=pl.CostEstimate(flops=1 << 18, bytes_accessed=1 << 18, transcendentals=256),
-        compiler_params=pltpu.CompilerParams(vmem_limit_bytes=8 << 20),
-        name="final",
-    )(mixed, own, back)
+    )(far(y), far(cum), enter, far(decay_log), far(out_map), far(mixer_weight), own, back)
 
 
 def scores_kernel(pos_ref, q_ref, p_ref, k0_ref, k1_ref, k2_ref, away_ref, stat_ref, raw, w_ref, sems):
@@ -410,7 +397,8 @@
     def fetch(h):
         return pltpu.make_async_copy(away_ref.at[h, pl.ds(*rows), :], w_ref.at[h], sems.at[h])
 
-    for h in range(HEADS):
+    ahead = 3
+    for h in range(ahead):
         fetch(h).start()
     side = lax.rem(pos_ref[0], 2)
     at = lambda ref, k: (ref[k * 8 : k * 8 + 8, :], ref[k * 8 + 8 : k * 8 + 16, :])
@@ -426,6 +414,11 @@
         scale = jnp.sum(jnp.where(line == h, scale_s[...], 0.0), 0, keepdims=True)
         v0, v1, v2 = v0_ref[:, span], v1_ref[:, span], v2_ref[:, span]
         fetch(h).wait()
+
+        @pl.when(h + ahead < HEADS)
+        def _():
+            fetch(h + ahead).start()
+
         w = lambda n: w_ref[h, n * TOK : (n + 1) * TOK, :]
         if mine:
             taken = dot_0(v0, w(0)) + dot_0(v1, w(1)) + dot_0(v2, w(2))
@@ -435,7 +428,7 @@
         sum_s[...] += dot_0(weight_ref[span, :], (taken * scale).astype(BF16))
         return carry
 
-    lax.fori_loop(0, HEADS, head, 0, unroll=2)
+    lax.fori_loop(0, HEADS, head, 0)
     o_ref[...] = sum_s[...].astype(o_ref.dtype)
 
 
@@ -475,11 +468,11 @@
     other = swap(query_rows)
     k1 = shift(key_rows, 2)
     k2 = shift(key_rows, 4)
+    v1 = shift(value_rows, 2)
     y, cum, send, out_map = run_mixer(
         step_low, step_proj, step_bias, channels, decay_log, state_maps
     )
     got = lax.all_to_all(send, "ctx", 0, 0, tiled=True)
-    v1 = shift(value_rows, 2)
     v2 = shift(value_rows, 4)
     weights, stats = run_scores(position, query_rows, other, key_rows, k1, k2)
     given = run_prefix(position, got, decay_log)
@@ -489,9 +482,8 @@
     weights = pltpu.with_memory_space_constraint(weights, pltpu.HBM)
     give = run_values(False, position, weights, *blocks)
     back = swap(give)
-    mixed = run_enter(y, cum, enter, decay_log, out_map, mixer_weight)
     own = run_values(True, position, weights, *blocks)
-    return run_final(mixed, own, back)
+    return run_enter(y, cum, enter, decay_log, out_map, mixer_weight, own, back)
 
 
 def solution(mesh):

time: 132 us -> 129 us (0.977)
  Pallas kernels: 45.9 us -> 40.9 us
  waiting for transfers between devices: 28.2 us -> 30.8 us
    all_to_all x1, waiting for transfers between devices: 25.7 us -> 28.2 us  [per_device(): got = lax.all_to_all(send, 'ctx', 0, 0, tiled=True)]
    pallas_call x1, Pallas kernels: 11.8 us -> 9.83 us  [run_enter(): pl.pallas_call(enter_kernel, grid=(CH // CW,), in_specs=[blocked, blocked...]
    pallas_call x1, Pallas kernels: 16.4 us -> 14.5 us  [run_mixer(): pl.pallas_call(mixer_kernel, grid=(CH // CW,), in_specs=[fixed((TOK, 128)...]
  transfers between devices with their start and end apart: 9 -> 9, of which waited for: 2 -> 2; matrix products, arithmetic and copies ran while one was open for 0% -> 0% of each run, Pallas kernels for 34% -> 24%
where the time goes in v3:
time: 129 us; the launch traced here: 128 us
  starting transfers between devices  56.3 us (44%)
  Pallas kernels  40.9 us (32%)
  waiting for transfers between devices  30.8 us (24%)
    all_to_all x1, waiting for transfers between devices, per_device(): got = lax.all_to_all(send, 'ctx', 0, 0, tiled=True)  28.2 us
    ppermute x3, starting transfers between devices, swap(): return lax.ppermute(value, 'ctx', [(s, s ^ 1) for s in range(N_CTX)])  25.5 us
    ppermute x4, starting transfers between devices, shift(): lax.ppermute(value, 'ctx', [(s, s + steps) for s in range(N_CTX - steps)])  15.5 us
    pallas_call x1, Pallas kernels, run_mixer(): pl.pallas_call(mixer_kernel, grid=(CH // CW,), in_specs=[fixed((TOK, 128)...  14.5 us
    pallas_call x1, Pallas kernels, run_enter(): pl.pallas_call(enter_kernel, grid=(CH // CW,), in_specs=[blocked, blocked...  9.83 us
    pallas_call x2, Pallas kernels, run_values(): pl.pallas_call(functools.partial(values_kernel, mine), in_specs=[SMEM, AW...  9.25 us
    all_to_all x1, starting transfers between devices, per_device(): got = lax.all_to_all(send, 'ctx', 0, 0, tiled=True)  8.2 us
    all_to_all x1, starting transfers between devices, per_device(): enter = lax.all_to_all(given, 'ctx', 0, 0, tiled=True)  7.11 us
  transfers between devices with their start and end apart: 9, of which 2 were waited for; matrix products, arithmetic and copies ran while one was open for 0% of the time, Pallas kernels for 24%

profile of v3, /device:TPU:2, one launch (start us, length us, event | category | flops | bytes accessed | tf_op | source)
XLA Modules:
  0.0 128.2 jit_solution(2271127364009661663)
XLA Ops:
  0.0 3.4 %collective-permute-start.1 = (bf16[256,1024]{1,0:T(8,128)(2,1)}, bf16[256,1024]{1,0:T(8,128)(2,1)S(1)}, u32[]{:S(2)}, u32[]{:S(2)}) collective-permute-start(bf16[256,1024]{1,0:T(8,128)(2,1)} %k0_ref.1), channel_id=1, source_target_pairs={{0,16},{8,24},{16,32},{24,40},{32,48},{40,56},{48,64},{56,72},{64,... | collective-permute-start | bytes 1572872 | tf_op jit(solution)/shard_map/ppermute | solution.py:456
  3.4 4.1 %collective-permute-start.2 = (bf16[256,1024]{1,0:T(8,128)(2,1)}, bf16[256,1024]{1,0:T(8,128)(2,1)S(1)}, u32[]{:S(2)}, u32[]{:S(2)}) collective-permute-start(bf16[256,1024]{1,0:T(8,128)(2,1)} %k0_ref.1), channel_id=1, source_target_pairs={{0,32},{8,40},{16,48},{24,56},{32,64},{40,72},{48,80},{56,88},{64,... | collective-permute-start | bytes 1572872 | tf_op jit(solution)/shard_map/ppermute | solution.py:456
  7.5 2.8 %collective-permute-start.3 = (bf16[256,1024]{1,0:T(8,128)(2,1)}, bf16[256,1024]{1,0:T(8,128)(2,1)S(1)}, u32[]{:S(2)}, u32[]{:S(2)}) collective-permute-start(bf16[256,1024]{1,0:T(8,128)(2,1)} %v0_ref.3), channel_id=1, source_target_pairs={{0,16},{8,24},{16,32},{24,40},{32,48},{40,56},{48,64},{56,72},{64,... | collective-permute-start | bytes 1572872 | tf_op jit(solution)/shard_map/ppermute | solution.py:456
  10.2 5.3 %collective-permute-start.4 = (bf16[256,1024]{1,0:T(8,128)(2,1)}, bf16[256,1024]{1,0:T(8,128)(2,1)S(1)}, u32[]{:S(2)}, u32[]{:S(2)}) collective-permute-start(bf16[256,1024]{1,0:T(8,128)(2,1)} %v0_ref.3), channel_id=1, source_target_pairs={{0,32},{8,40},{16,48},{24,56},{32,64},{40,72},{48,80},{56,88},{64,... | collective-permute-start | bytes 1572872 | tf_op jit(solution)/shard_map/ppermute | solution.py:456
  15.5 10.9 %collective-permute-start = (bf16[256,1024]{1,0:T(8,128)(2,1)}, bf16[256,1024]{1,0:T(8,128)(2,1)}, u32[]{:S(2)}, u32[]{:S(2)}) collective-permute-start(bf16[256,1024]{1,0:T(8,128)(2,1)} %q_ref.1), channel_id=1, source_target_pairs={{0,8},{8,0},{16,24},{24,16},{32,40},{40,32},{48,56},{56,48},{64,72... | collective-permute-start | bytes 1572872 | tf_op jit(solution)/shard_map/ppermute | solution.py:460
  26.4 0.0 copy-start.2
  26.5 0.0 copy-start.3
  26.5 0.0 copy-start.4
  26.5 14.5 %mixer.1 = (f32[16,16,2048]{2,1,0:T(8,128)}, f32[16,16,2048]{2,1,0:T(8,128)}, bf16[64,8,128]{2,1,0:T(8,128)(2,1)}, bf16[16,32,256]{2,1,0:T(8,128)(2,1)}) custom-call(bf16[256,128]{1,0:T(8,128)(2,1)} %low_ref.1, bf16[128,2048]{1,0:T(8,128)(2,1)} %proj_ref.1, f32[1,2048]{1,0:T(1,128)} %bitcast.2, bf16[256,2048]{1,0:T(8,128)(2,1)} %chan_ref.1, ...), custom_call_target="tpu_custom_call" | custom-call | flops 6000000000 | bytes 8388608 | tf_op jit(solution)/shard_map/mixer/pallas_call | solution.py:142
  40.9 8.2 %all-to-all-start = ((bf16[64,8,128]{2,1,0:T(8,128)(2,1)}), bf16[64,8,128]{2,1,0:T(8,128)(2,1)S(1)}, u32[]{:S(2)}, u32[]{:S(2)}) async-start(bf16[64,8,128]{2,1,0:T(8,128)(2,1)} %get-tuple-element.13), calls=%async_computation | async-start | bytes 262144 | tf_op jit(solution)/shard_map/all_to_all | solution.py:475
  49.2 28.2 %all-to-all-done.got_ref = bf16[64,8,128]{2,1,0:T(8,128)(2,1)S(1)} async-done(((bf16[64,8,128]{2,1,0:T(8,128)(2,1)}), bf16[64,8,128]{2,1,0:T(8,128)(2,1)S(1)}, u32[]{:S(2)}, u32[]{:S(2)}) %all-to-all-start) | async-done | bytes 131104 | tf_op jit(solution)/shard_map/all_to_all | solution.py:475
  77.4 0.0 copy-done.2
  77.4 0.8 prefix.1
  78.2 7.1 %all-to-all-start.1 = ((f32[64,4,128]{2,1,0:T(4,128)}), f32[64,4,128]{2,1,0:T(4,128)S(1)}, u32[]{:S(2)}, u32[]{:S(2)}) async-start(f32[64,4,128]{2,1,0:T(4,128)} %prefix.1), calls=%async_computation.1 | async-start | bytes 262144 | tf_op jit(solution)/shard_map/all_to_all | solution.py:479
  85.3 0.0 copy-start
  85.4 0.0 copy-start.1
  85.4 0.0 collective-permute-done.p_ref
  85.4 0.0 collective-permute-done.1.k1_ref
  85.4 0.0 collective-permute-done.2.k2_ref
  85.4 0.0 copy-done.3
  85.4 6.5 %scores.1 = (bf16[8,1280,256]{2,1,0:T(8,128)(2,1)}, f32[32,256]{1,0:T(8,128)S(1)}) custom-call(s32[1]{0:T(128)} %bitcast.1.pos_ref, bf16[256,1024]{1,0:T(8,128)(2,1)S(1)} %copy-done.3, bf16[256,1024]{1,0:T(8,128)(2,1)} %collective-permute-done.p_ref, bf16[256,1024]{1,0:T(8,128)(2,1)S(1)} %copy-done.4, bf16[256,1024]{1,0:T(8,128)(2,1)S(1)} %collective-permute-done.1.k1_ref, ...), custom_call_target="tpu_custom_call" | custom-call | flops 700000000 | bytes 8388608 | tf_op jit(solution)/shard_map/scores/pallas_call | solution.py:366
  92.0 7.3 %collective-permute-start.5 = (f32[32,256]{1,0:T(8,128)S(1)}, f32[32,256]{1,0:T(8,128)S(1)}, u32[]{:S(2)}, u32[]{:S(2)}) collective-permute-start(f32[32,256]{1,0:T(8,128)S(1)} %get-tuple-element.16.stat_ref), channel_id=1, source_target_pairs={{0,8},{8,0},{16,24},{24,16},{32,40},{40,32},{48,56},{56,48},{64,72... | collective-permute-start | bytes 98312 | tf_op jit(solution)/shard_map/ppermute | solution.py:460
  99.2 0.0 collective-permute-done.3.v1_ref
  99.3 0.0 collective-permute-done.4.v2_ref
  99.3 2.5 %collective-permute-done.5.got_ref = f32[32,256]{1,0:T(8,128)S(1)} collective-permute-done((f32[32,256]{1,0:T(8,128)S(1)}, f32[32,256]{1,0:T(8,128)S(1)}, u32[]{:S(2)}, u32[]{:S(2)}) %collective-permute-start.5) | collective-permute-done | bytes 32800 | tf_op jit(solution)/shard_map/ppermute | solution.py:460
  101.8 0.0 copy-done
  101.8 4.6 %values_other.1 = bf16[128,256]{1,0:T(8,128)(2,1)S(1)} custom-call(s32[1]{0:T(128)} %bitcast.1.pos_ref, bf16[8,1280,256]{2,1,0:T(8,128)(2,1)} %get-tuple-element.15.away_ref, bf16[256,1024]{1,0:T(8,128)(2,1)S(1)} %copy-done, bf16[256,1024]{1,0:T(8,128)(2,1)S(1)} %collective-permute-done.3.v1_ref, bf16[256,1024]{1,0:T(8,128)(2,1)S(1)} %collective-permute-done.4.v2_ref, ...), custom_call_target="tpu_custom_call" | custom-call | flops 400000000 | bytes 4194304 | tf_op jit(solution)/shard_map/values_other/pallas_call | solution.py:436
  106.4 7.3 %collective-permute-start.6 = (bf16[128,256]{1,0:T(8,128)(2,1)S(1)}, bf16[128,256]{1,0:T(8,128)(2,1)S(1)}, u32[]{:S(2)}, u32[]{:S(2)}) collective-permute-start(bf16[128,256]{1,0:T(8,128)(2,1)S(1)} %values_other.1), channel_id=1, source_target_pairs={{0,8},{8,0},{16,24},{24,16},{32,40},{40,32},{48,56},{56,48},{64,72... | collective-permute-start | bytes 196616 | tf_op jit(solution)/shard_map/ppermute | solution.py:460
  113.6 4.7 %values_own.1.own_ref = f32[128,256]{1,0:T(8,128)S(1)} custom-call(s32[1]{0:T(128)} %bitcast.1.pos_ref, bf16[8,1280,256]{2,1,0:T(8,128)(2,1)} %get-tuple-element.15.away_ref, bf16[256,1024]{1,0:T(8,128)(2,1)S(1)} %copy-done, bf16[256,1024]{1,0:T(8,128)(2,1)S(1)} %collective-permute-done.3.v1_ref, bf16[256,1024]{1,0:T(8,128)(2,1)S(1)} %collective-permute-done.4.v2_ref, ...), custom_call_target="tpu_custom_call" | custom-call | flops 400000000 | bytes 4194304 | tf_op jit(solution)/shard_map/values_own/pallas_call | solution.py:436
  118.3 0.0 all-to-all-done.1.enter_ref
  118.3 0.0 collective-permute-done.6.back_ref
  118.3 9.8 %enter.1 = bf16[256,128]{1,0:T(8,128)(2,1)} custom-call(f32[16,16,2048]{2,1,0:T(8,128)} %get-tuple-element.11.y_ref, f32[16,16,2048]{2,1,0:T(8,128)} %get-tuple-element.12.cum_ref, f32[64,4,128]{2,1,0:T(4,128)S(1)} %all-to-all-done.1.enter_ref, f32[16,2048]{1,0:T(8,128)} %log_ref.5, bf16[16,32,256]{2,1,0:T(8,128)(2,1)} %get-tuple-element.14.out_ref, ...), custom_call_target="tpu_custom_call" | custom-call | flops 4000000000 | bytes 6291456 | tf_op jit(solution)/shard_map/enter/pallas_call | solution.py:255
  (2 shorter events, 0.0 us)
Async XLA Ops:
  0.0 85.4 %collective-permute-start.1 = (bf16[256,1024]{1,0:T(8,128)(2,1)}, bf16[256,1024]{1,0:T(8,128)(2,1)S(1)}, u32[]{:S(2)}, u32[]{:S(2)}) collective-permute-start(bf16[256,1024]{1,0:T(8,128)(2,1)} %k0_ref.1), channel_id=1, source_target_pairs={{0,16},{8,24},{16,32},{24,40},{32,48},{40,56},{48,64},{56,72},{64,... | collective-permute-start | bytes 1572872 | tf_op jit(solution)/shard_map/ppermute | solution.py:456
  3.4 82.0 %collective-permute-start.2 = (bf16[256,1024]{1,0:T(8,128)(2,1)}, bf16[256,1024]{1,0:T(8,128)(2,1)S(1)}, u32[]{:S(2)}, u32[]{:S(2)}) collective-permute-start(bf16[256,1024]{1,0:T(8,128)(2,1)} %k0_ref.1), channel_id=1, source_target_pairs={{0,32},{8,40},{16,48},{24,56},{32,64},{40,72},{48,80},{56,88},{64,... | collective-permute-start | bytes 1572872 | tf_op jit(solution)/shard_map/ppermute | solution.py:456
  7.5 91.8 %collective-permute-start.3 = (bf16[256,1024]{1,0:T(8,128)(2,1)}, bf16[256,1024]{1,0:T(8,128)(2,1)S(1)}, u32[]{:S(2)}, u32[]{:S(2)}) collective-permute-start(bf16[256,1024]{1,0:T(8,128)(2,1)} %v0_ref.3), channel_id=1, source_target_pairs={{0,16},{8,24},{16,32},{24,40},{32,48},{40,56},{48,64},{56,72},{64,... | collective-permute-start | bytes 1572872 | tf_op jit(solution)/shard_map/ppermute | solution.py:456
  10.2 89.0 %collective-permute-start.4 = (bf16[256,1024]{1,0:T(8,128)(2,1)}, bf16[256,1024]{1,0:T(8,128)(2,1)S(1)}, u32[]{:S(2)}, u32[]{:S(2)}) collective-permute-start(bf16[256,1024]{1,0:T(8,128)(2,1)} %v0_ref.3), channel_id=1, source_target_pairs={{0,32},{8,40},{16,48},{24,56},{32,64},{40,72},{48,80},{56,88},{64,... | collective-permute-start | bytes 1572872 | tf_op jit(solution)/shard_map/ppermute | solution.py:456
  15.5 69.9 %collective-permute-start = (bf16[256,1024]{1,0:T(8,128)(2,1)}, bf16[256,1024]{1,0:T(8,128)(2,1)}, u32[]{:S(2)}, u32[]{:S(2)}) collective-permute-start(bf16[256,1024]{1,0:T(8,128)(2,1)} %q_ref.1), channel_id=1, source_target_pairs={{0,8},{8,0},{16,24},{24,16},{32,40},{40,32},{48,56},{56,48},{64,72... | collective-permute-start | bytes 1572872 | tf_op jit(solution)/shard_map/ppermute | solution.py:460
  26.4 51.0 %copy-start.2 = (f32[16,2048]{1,0:T(8,128)S(1)}, f32[16,2048]{1,0:T(8,128)}, u32[]{:S(2)}) copy-start(f32[16,2048]{1,0:T(8,128)} %log_ref.5) | copy-start | bytes 393220
  26.5 58.9 %copy-start.3 = (bf16[256,1024]{1,0:T(8,128)(2,1)S(1)}, bf16[256,1024]{1,0:T(8,128)(2,1)}, u32[]{:S(2)}) copy-start(bf16[256,1024]{1,0:T(8,128)(2,1)} %q_ref.1) | copy-start | bytes 1572868
  26.5 58.9 %copy-start.4 = (bf16[256,1024]{1,0:T(8,128)(2,1)S(1)}, bf16[256,1024]{1,0:T(8,128)(2,1)}, u32[]{:S(2)}) copy-start(bf16[256,1024]{1,0:T(8,128)(2,1)} %k0_ref.1) | copy-start | bytes 1572868
  40.9 36.5 %all-to-all-start = ((bf16[64,8,128]{2,1,0:T(8,128)(2,1)}), bf16[64,8,128]{2,1,0:T(8,128)(2,1)S(1)}, u32[]{:S(2)}, u32[]{:S(2)}) async-start(bf16[64,8,128]{2,1,0:T(8,128)(2,1)} %get-tuple-element.13), calls=%async_computation | async-start | bytes 262144 | tf_op jit(solution)/shard_map/all_to_all | solution.py:475
  78.2 40.1 %all-to-all-start.1 = ((f32[64,4,128]{2,1,0:T(4,128)}), f32[64,4,128]{2,1,0:T(4,128)S(1)}, u32[]{:S(2)}, u32[]{:S(2)}) async-start(f32[64,4,128]{2,1,0:T(4,128)} %prefix.1), calls=%async_computation.1 | async-start | bytes 262144 | tf_op jit(solution)/shard_map/all_to_all | solution.py:479
  85.3 16.4 %copy-start = (bf16[256,1024]{1,0:T(8,128)(2,1)S(1)}, bf16[256,1024]{1,0:T(8,128)(2,1)}, u32[]{:S(2)}) copy-start(bf16[256,1024]{1,0:T(8,128)(2,1)} %v0_ref.3) | copy-start | bytes 1572868
  85.4 16.4 %copy-start.1 = (bf16[1024,128]{1,0:T(8,128)(2,1)S(1)}, bf16[1024,128]{1,0:T(8,128)(2,1)}, u32[]{:S(2)}) copy-start(bf16[1024,128]{1,0:T(8,128)(2,1)} %weight_ref.4) | copy-start | bytes 786436
  92.0 9.8 %collective-permute-start.5 = (f32[32,256]{1,0:T(8,128)S(1)}, f32[32,256]{1,0:T(8,128)S(1)}, u32[]{:S(2)}, u32[]{:S(2)}) collective-permute-start(f32[32,256]{1,0:T(8,128)S(1)} %get-tuple-element.16.stat_ref), channel_id=1, source_target_pairs={{0,8},{8,0},{16,24},{24,16},{32,40},{40,32},{48,56},{56,48},{64,72... | collective-permute-start | bytes 98312 | tf_op jit(solution)/shard_map/ppermute | solution.py:460
  106.4 12.0 %collective-permute-start.6 = (bf16[128,256]{1,0:T(8,128)(2,1)S(1)}, bf16[128,256]{1,0:T(8,128)(2,1)S(1)}, u32[]{:S(2)}, u32[]{:S(2)}) collective-permute-start(bf16[128,256]{1,0:T(8,128)(2,1)S(1)} %values_other.1), channel_id=1, source_target_pairs={{0,8},{8,0},{16,24},{24,16},{32,40},{40,32},{48,56},{56,48},{64,72... | collective-permute-start | bytes 196616 | tf_op jit(solution)/shard_map/ppermute | solution.py:460

commit v4 on v3

--- a/solution.py
+++ b/solution.py
@@ -48,31 +48,53 @@
     return jnp.maximum(v, 0.0) + jnp.log1p(jnp.exp(-jnp.abs(v)))
 
 
-def mixer_kernel(
+def mixer_first_kernel(pos_ref, *refs):
+    @pl.when(lax.rem(pos_ref[0], 2) == 0)
+    def _():
+        mixer_tables(*refs)
+        mixer_chunk(*refs)
+
+
+def mixer_rest_kernel(pos_ref, *refs):
+    refs = refs[:6] + refs[9:]
+
+    @pl.when(pl.program_id(0) == 0)
+    def _():
+        mixer_tables(*refs)
+
+    @pl.when((pl.program_id(0) > 0) | (lax.rem(pos_ref[0], 2) == 1))
+    def _():
+        mixer_chunk(*refs)
+
+
+def mixer_tables(
+    low_ref, proj_ref, bias_ref, chan_ref, log_ref, maps_ref,
+    y_ref, cum_ref, send_ref, out_ref,
+    step_s, flow_s, in_s,
+):
+    in_map = maps_ref[0]
+    for t in range(TOK):
+        in_s[t] = jnp.broadcast_to(in_map[:, t : t + 1], (NS, LANES))
+    spread = (
+        lax.broadcasted_iota(jnp.int32, (NS, BLK * NS), 1) % NS
+        == lax.broadcasted_iota(jnp.int32, (NS, BLK * NS), 0)
+    ).astype(F32).astype(BF16)
+    keep = (
+        lax.broadcasted_iota(jnp.int32, (TOK, BLK * NS), 1) // NS
+        == lax.broadcasted_iota(jnp.int32, (TOK, BLK * NS), 0) % BLK
+    )
+    hi, mid, _ = pieces(jnp.transpose(maps_ref[1]))
+    for k, piece in enumerate((hi, mid)):
+        rows = jnp.where(keep, dot(piece, spread), 0.0).astype(BF16)
+        out_ref[:, k * BLK : (k + 1) * BLK, :] = rows.reshape(TOK // BLK, BLK, BLK * NS)
+
+
+def mixer_chunk(
     low_ref, proj_ref, bias_ref, chan_ref, log_ref, maps_ref,
     y_ref, cum_ref, send_ref, out_ref,
     step_s, flow_s, in_s,
 ):
     groups = CW // LANES
-
-    @pl.when(pl.program_id(0) == 0)
-    def _():
-        in_map = maps_ref[0]
-        for t in range(TOK):
-            in_s[t] = jnp.broadcast_to(in_map[:, t : t + 1], (NS, LANES))
-        spread = (
-            lax.broadcasted_iota(jnp.int32, (NS, BLK * NS), 1) % NS
-            == lax.broadcasted_iota(jnp.int32, (NS, BLK * NS), 0)
-        ).astype(F32).astype(BF16)
-        keep = (
-            lax.broadcasted_iota(jnp.int32, (TOK, BLK * NS), 1) // NS
-            == lax.broadcasted_iota(jnp.int32, (TOK, BLK * NS), 0) % BLK
-        )
-        hi, mid, _ = pieces(jnp.transpose(maps_ref[1]))
-        for k, piece in enumerate((hi, mid)):
-            rows = jnp.where(keep, dot(piece, spread), 0.0).astype(BF16)
-            out_ref[:, k * BLK : (k + 1) * BLK, :] = rows.reshape(TOK // BLK, BLK, BLK * NS)
-
     rows = 64
     part = rows // BLK
     half = 2 * LANES
@@ -134,42 +156,59 @@
             ).astype(BF16)
 
 
-def run_mixer(step_low, step_proj, step_bias, channels, decay_log, state_maps):
+def run_mixer(position, step_low, step_proj, step_bias, channels, decay_log, state_maps, begun=None):
     blocked = (TOK // BLK, BLK, CW)
     whole = jax.ShapeDtypeStruct((TOK // BLK, BLK, CH), F32)
     out_map = (TOK // BLK, 2 * BLK, BLK * NS)
-    fixed = lambda shape: pl.BlockSpec(shape, lambda i: (0,) * len(shape))
+    first = begun is None
+    if first:
+        chunk = lambda i, pos: 0
+    else:
+        chunk = lambda i, pos: jnp.where(lax.rem(pos[0], 2) == 0, jnp.maximum(i, 1), i)
+    fixed = lambda shape: pl.BlockSpec(shape, lambda i, pos: (0,) * len(shape))
+    out_specs = [
+        pl.BlockSpec(blocked, lambda i, pos: (0, 0, chunk(i, pos))),
+        pl.BlockSpec(blocked, lambda i, pos: (0, 0, chunk(i, pos))),
+        pl.BlockSpec((CW // LANES * 4, 8, LANES), lambda i, pos: (chunk(i, pos), 0, 0)),
+    ]
+    out_shape = [whole, whole, jax.ShapeDtypeStruct((N_CTX, 8, LANES), BF16)]
+    scratch = [
+        pltpu.VMEM(blocked, F32),
+        pltpu.VMEM(blocked, F32),
+        pltpu.VMEM((TOK, NS, LANES), F32),
+    ]
+    if first:
+        scratch = [pltpu.VMEM(out_map, BF16)] + scratch
+    else:
+        out_specs = out_specs + [fixed(out_map)]
+        out_shape = out_shape + [jax.ShapeDtypeStruct(out_map, BF16)]
     return pl.pallas_call(
-        mixer_kernel,
-        grid=(CH // CW,),
-        in_specs=[
-            fixed((TOK, 128)),
-            pl.BlockSpec((128, CW), lambda i: (0, i)),
-            pl.BlockSpec((1, CW), lambda i: (0, i)),
-            pl.BlockSpec((TOK, CW), lambda i: (0, i)),
-            pl.BlockSpec((NS, CW), lambda i: (0, i)),
-            fixed((2, NS, TOK)),
-        ],
-        out_specs=[
-            pl.BlockSpec(blocked, lambda i: (0, 0, i)),
-            pl.BlockSpec(blocked, lambda i: (0, 0, i)),
-            pl.BlockSpec((CW // LANES * 4, 8, LANES), lambda i: (i, 0, 0)),
-            fixed(out_map),
-        ],
-        out_shape=[
-            whole, whole, jax.ShapeDtypeStruct((N_CTX, 8, LANES), BF16),
-            jax.ShapeDtypeStruct(out_map, BF16),
-        ],
-        scratch_shapes=[
-            pltpu.VMEM(blocked, F32),
-            pltpu.VMEM(blocked, F32),
-            pltpu.VMEM((TOK, NS, LANES), F32),
-        ],
+        mixer_first_kernel if first else mixer_rest_kernel,
+        grid_spec=pltpu.PrefetchScalarGridSpec(
+            num_scalar_prefetch=1,
+            grid=(1 if first else CH // CW,),
+            in_specs=[
+                fixed((TOK, 128)),
+                pl.BlockSpec((128, CW), lambda i, pos: (0, chunk(i, pos))),
+                pl.BlockSpec((1, CW), lambda i, pos: (0, chunk(i, pos))),
+                pl.BlockSpec((TOK, CW), lambda i, pos: (0, chunk(i, pos))),
+                pl.BlockSpec((NS, CW), lambda i, pos: (0, chunk(i, pos))),
+                fixed((2, NS, TOK)),
+            ]
+            + ([] if first else [pl.BlockSpec(memory_space=pl.ANY)] * 3),
+            out_specs=out_specs,
+            scratch_shapes=scratch,
+        ),
+        out_shape=out_shape,
+        input_output_aliases={} if first else {7: 0, 8: 1, 9: 2},
         cost_estimate=pl.CostEstimate(
-            flops=6_000_000_000, bytes_accessed=8 << 20, transcendentals=8 << 20
+            flops=(1 if first else 5) * 1_000_000_000, bytes_accessed=8 << 20, transcendentals=8 << 20
         ),
-        name="mixer",
-    )(step_low, step_proj, step_bias.reshape(1, CH), channels, decay_log, state_maps)
+        name="mixer_first" if first else "mixer_rest",
+    )(
+        position, step_low, step_proj, step_bias.reshape(1, CH), channels, decay_log, state_maps,
+        *(begun or ()),
+    )
 
 
 def prefix_kernel(pos_ref, got_ref, log_ref, out_ref):
@@ -276,18 +315,27 @@
     )(far(y), far(cum), enter, far(decay_log), far(out_map), far(mixer_weight), own, back)
 
 
-def scores_kernel(pos_ref, q_ref, p_ref, k0_ref, k1_ref, k2_ref, away_ref, stat_ref, raw, w_ref, sems):
+def scores_kernel(
+    pos_ref, q_ref, p_ref, k0_ref, k1_ref, k2_ref, own_ref, other_ref, stat_ref, raw, w_ref, sems,
+):
     def out(h):
-        return pltpu.make_async_copy(w_ref.at[h], away_ref.at[h], sems.at[h])
+        mine = w_ref.at[h, pl.ds(0, 3 * TOK), :]
+        other = w_ref.at[h, pl.ds(3 * TOK, 2 * TOK), :]
+        return (
+            pltpu.make_async_copy(mine, own_ref.at[h], sems.at[0, h]),
+            pltpu.make_async_copy(other, other_ref.at[h], sems.at[1, h]),
+        )
 
     def head(h, carry):
         scores_head(h, pos_ref, q_ref, p_ref, k0_ref, k1_ref, k2_ref, w_ref, stat_ref, raw)
-        out(h).start()
+        for copy in out(h):
+            copy.start()
         return carry
 
     lax.fori_loop(0, HEADS, head, 0)
     for h in range(HEADS):
-        out(h).wait()
+        for copy in out(h):
+            copy.wait()
 
 
 def scores_head(h, pos_ref, q_ref, p_ref, k0_ref, k1_ref, k2_ref, w_ref, stat_ref, raw):
@@ -366,14 +414,15 @@
     return pl.pallas_call(
         scores_kernel,
         in_specs=[SMEM] + [VMEM] * 5,
-        out_specs=[AWAY, VMEM],
+        out_specs=[AWAY, AWAY, VMEM],
         scratch_shapes=[
             pltpu.VMEM((5 * TOK, TOK), F32),
             pltpu.VMEM((HEADS, 5 * TOK, TOK), BF16),
-            pltpu.SemaphoreType.DMA((HEADS,)),
+            pltpu.SemaphoreType.DMA((2, HEADS)),
         ],
         out_shape=[
-            pltpu.HBM((HEADS, 5 * TOK, TOK), BF16),
+            pltpu.HBM((HEADS, 3 * TOK, TOK), BF16),
+            pltpu.HBM((HEADS, 2 * TOK, TOK), BF16),
             jax.ShapeDtypeStruct((4 * HEADS, TOK), F32),
         ],
         compiler_params=pltpu.CompilerParams(vmem_limit_bytes=16 << 20),
@@ -381,7 +430,7 @@
             flops=700_000_000, bytes_accessed=8 << 20, transcendentals=3 << 20
         ),
         name="scores",
-    )(position, query, other, k0, k1, k2)
+    )(position, pltpu.with_memory_space_constraint(query, pltpu.HBM), other, pltpu.with_memory_space_constraint(k0, pltpu.HBM), k1, k2)
 
 
 def dot_0(a, b):
@@ -389,17 +438,9 @@
 
 
 def values_kernel(
-    mine, pos_ref, away_ref, v0_ref, v1_ref, v2_ref, stat_ref, got_ref, weight_ref, o_ref,
-    scale_s, sum_s, w_ref, sems,
+    mine, pos_ref, w_ref, v0_ref, v1_ref, v2_ref, stat_ref, got_ref, weight_ref, o_ref,
+    scale_s, sum_s,
 ):
-    rows = (0, 3 * TOK) if mine else (3 * TOK, 2 * TOK)
-
-    def fetch(h):
-        return pltpu.make_async_copy(away_ref.at[h, pl.ds(*rows), :], w_ref.at[h], sems.at[h])
-
-    ahead = 3
-    for h in range(ahead):
-        fetch(h).start()
     side = lax.rem(pos_ref[0], 2)
     at = lambda ref, k: (ref[k * 8 : k * 8 + 8, :], ref[k * 8 + 8 : k * 8 + 16, :])
     (m0, l0), (m1, l1) = at(stat_ref, 0 if mine else 2), at(got_ref, 2 if mine else 0)
@@ -413,12 +454,6 @@
         span = pl.ds(pl.multiple_of(h * HD, HD), HD)
         scale = jnp.sum(jnp.where(line == h, scale_s[...], 0.0), 0, keepdims=True)
         v0, v1, v2 = v0_ref[:, span], v1_ref[:, span], v2_ref[:, span]
-        fetch(h).wait()
-
-        @pl.when(h + ahead < HEADS)
-        def _():
-            fetch(h + ahead).start()
-
         w = lambda n: w_ref[h, n * TOK : (n + 1) * TOK, :]
         if mine:
             taken = dot_0(v0, w(0)) + dot_0(v1, w(1)) + dot_0(v2, w(2))
@@ -435,13 +470,11 @@
 def run_values(mine, position, weights, v0, v1, v2, stats, got, attend_weight):
     return pl.pallas_call(
         functools.partial(values_kernel, mine),
-        in_specs=[SMEM, AWAY] + [VMEM] * 6,
+        in_specs=[SMEM] + [VMEM] * 7,
         out_specs=VMEM,
         scratch_shapes=[
             pltpu.VMEM((HEADS, TOK), F32),
             pltpu.VMEM((EMB, TOK), F32),
-            pltpu.VMEM((HEADS, (3 if mine else 2) * TOK, TOK), BF16),
-            pltpu.SemaphoreType.DMA((HEADS,)),
         ],
         out_shape=jax.ShapeDtypeStruct((EMB, TOK), F32 if mine else BF16),
         compiler_params=pltpu.CompilerParams(vmem_limit_bytes=16 << 20),
@@ -465,24 +498,25 @@
     state_maps, attend_weight, mixer_weight,
 ):
     position = lax.axis_index("ctx").astype(jnp.int32).reshape(1)
+    mixer_args = (
+        position, step_low, step_proj, step_bias, channels, decay_log, state_maps
+    )
+    begun = run_mixer(*mixer_args)
     other = swap(query_rows)
     k1 = shift(key_rows, 2)
     k2 = shift(key_rows, 4)
     v1 = shift(value_rows, 2)
-    y, cum, send, out_map = run_mixer(
-        step_low, step_proj, step_bias, channels, decay_log, state_maps
-    )
+    y, cum, send, out_map = run_mixer(*mixer_args, begun)
     got = lax.all_to_all(send, "ctx", 0, 0, tiled=True)
+    w_own, w_other, stats = run_scores(position, query_rows, other, key_rows, k1, k2)
     v2 = shift(value_rows, 4)
-    weights, stats = run_scores(position, query_rows, other, key_rows, k1, k2)
     given = run_prefix(position, got, decay_log)
     enter = lax.all_to_all(given, "ctx", 0, 0, tiled=True)
     got_stats = swap(stats)
     blocks = (value_rows, v1, v2, stats, got_stats, attend_weight)
-    weights = pltpu.with_memory_space_constraint(weights, pltpu.HBM)
-    give = run_values(False, position, weights, *blocks)
+    give = run_values(False, position, w_other, *blocks)
     back = swap(give)
-    own = run_values(True, position, weights, *blocks)
+    own = run_values(True, position, w_own, *blocks)
     return run_enter(y, cum, enter, decay_log, out_map, mixer_weight, own, back)
 
 

time: 129 us -> 124 us (0.961)
  the two profiles are of different devices: /device:TPU:2 before, /device:TPU:6 now
where the time goes in v4:
time: 124 us; the launch traced here: 123 us
  starting transfers between devices  48.1 us (39%)
  Pallas kernels  41.3 us (33%)
  blocking collectives  29.5 us (24%)
  waiting for transfers between devices  2.52 us (2%)
  local copies, waits for them, and re-layouts  1.61 us (1%)
    all_to_all x1, blocking collectives, per_device(): got = lax.all_to_all(send, 'ctx', 0, 0, tiled=True)  29.5 us
    ppermute x3, starting transfers between devices, swap(): return lax.ppermute(value, 'ctx', [(s, s ^ 1) for s in range(N_CTX)])  26 us
    pallas_call x2, Pallas kernels, run_mixer(): pl.pallas_call(mixer_first_kernel if first else mixer_rest_kernel, grid_s...  17.2 us
    ppermute x4, starting transfers between devices, shift(): lax.ppermute(value, 'ctx', [(s, s + steps) for s in range(N_CTX - steps)])  15.2 us
    pallas_call x1, Pallas kernels, run_enter(): pl.pallas_call(enter_kernel, grid=(CH // CW,), in_specs=[blocked, blocked...  9.83 us
    all_to_all x1, starting transfers between devices, per_device(): enter = lax.all_to_all(given, 'ctx', 0, 0, tiled=True)  6.97 us
    pallas_call x1, Pallas kernels, run_scores(): pl.pallas_call(scores_kernel, in_specs=[SMEM] + [VMEM] * 5, out_specs=[AW...  6.79 us
    pallas_call x2, Pallas kernels, run_values(): pl.pallas_call(functools.partial(values_kernel, mine), in_specs=[SMEM] +...  6.61 us
  transfers between devices with their start and end apart: 8, of which 1 were waited for; matrix products, arithmetic and copies ran while one was open for 0% of the time, Pallas kernels for 26%

profile of v4, /device:TPU:6, one launch (start us, length us, event | category | flops | bytes accessed | tf_op | source)
XLA Modules:
  0.0 123.2 jit_solution(5883745035049775299)
XLA Ops:
  0.0 3.4 %collective-permute-start.1 = (bf16[256,1024]{1,0:T(8,128)(2,1)}, bf16[256,1024]{1,0:T(8,128)(2,1)S(1)}, u32[]{:S(2)}, u32[]{:S(2)}) collective-permute-start(bf16[256,1024]{1,0:T(8,128)(2,1)} %k0_ref.1), channel_id=1, source_target_pairs={{0,16},{8,24},{16,32},{24,40},{32,48},{40,56},{48,64},{56,72},{64,... | collective-permute-start | bytes 1572872 | tf_op jit(solution)/shard_map/ppermute | solution.py:489
  3.4 4.3 %collective-permute-start.2 = (bf16[256,1024]{1,0:T(8,128)(2,1)}, bf16[256,1024]{1,0:T(8,128)(2,1)S(1)}, u32[]{:S(2)}, u32[]{:S(2)}) collective-permute-start(bf16[256,1024]{1,0:T(8,128)(2,1)} %k0_ref.1), channel_id=1, source_target_pairs={{0,32},{8,40},{16,48},{24,56},{32,64},{40,72},{48,80},{56,88},{64,... | collective-permute-start | bytes 1572872 | tf_op jit(solution)/shard_map/ppermute | solution.py:489
  7.7 4.0 %collective-permute-start.4 = (bf16[256,1024]{1,0:T(8,128)(2,1)}, bf16[256,1024]{1,0:T(8,128)(2,1)S(1)}, u32[]{:S(2)}, u32[]{:S(2)}) collective-permute-start(bf16[256,1024]{1,0:T(8,128)(2,1)} %v0_ref.3), channel_id=1, source_target_pairs={{0,32},{8,40},{16,48},{24,56},{32,64},{40,72},{48,80},{56,88},{64,... | collective-permute-start | bytes 1572872 | tf_op jit(solution)/shard_map/ppermute | solution.py:489
  11.8 3.4 %collective-permute-start.3 = (bf16[256,1024]{1,0:T(8,128)(2,1)}, bf16[256,1024]{1,0:T(8,128)(2,1)S(1)}, u32[]{:S(2)}, u32[]{:S(2)}) collective-permute-start(bf16[256,1024]{1,0:T(8,128)(2,1)} %v0_ref.3), channel_id=1, source_target_pairs={{0,16},{8,24},{16,32},{24,40},{32,48},{40,56},{48,64},{56,72},{64,... | collective-permute-start | bytes 1572872 | tf_op jit(solution)/shard_map/ppermute | solution.py:489
  15.2 10.9 %collective-permute-start = (bf16[256,1024]{1,0:T(8,128)(2,1)}, bf16[256,1024]{1,0:T(8,128)(2,1)S(1)}, u32[]{:S(2)}, u32[]{:S(2)}) collective-permute-start(bf16[256,1024]{1,0:T(8,128)(2,1)} %q_ref.1), channel_id=1, source_target_pairs={{0,8},{8,0},{16,24},{24,16},{32,40},{40,32},{48,56},{56,48},{64,72... | collective-permute-start | bytes 1572872 | tf_op jit(solution)/shard_map/ppermute | solution.py:493
  26.1 5.3 %mixer_first.1 = (f32[16,16,2048]{2,1,0:T(8,128)}, f32[16,16,2048]{2,1,0:T(8,128)}, bf16[64,8,128]{2,1,0:T(8,128)(2,1)}) custom-call(s32[1]{0:T(128)} %bitcast.pos_ref, bf16[256,128]{1,0:T(8,128)(2,1)} %refs_0_.3, bf16[128,2048]{1,0:T(8,128)(2,1)} %refs_1_.3, f32[1,2048]{1,0:T(1,128)} %bitcast.2, bf16[256,2048]{1,0:T(8,128)(2,1)} %refs_3_.3, ...), custom_call_target="tpu_custom_call" | custom-call | flops 1000000000 | bytes 8388608 | tf_op jit(solution)/shard_map/mixer_first/pallas_call | solution.py:185
  31.4 11.9 %mixer_rest.1 = (f32[16,16,2048]{2,1,0:T(8,128)}, f32[16,16,2048]{2,1,0:T(8,128)}, bf16[64,8,128]{2,1,0:T(8,128)(2,1)}, bf16[16,32,256]{2,1,0:T(8,128)(2,1)}) custom-call(s32[1]{0:T(128)} %bitcast.pos_ref, bf16[256,128]{1,0:T(8,128)(2,1)} %refs_0_.3, bf16[128,2048]{1,0:T(8,128)(2,1)} %refs_1_.3, ...), custom_call_target="tpu_custom_call", output_to_operand_aliasing={{0}: (7, {}), {1}: (8, {}), {2}: (9, {})} | custom-call | flops 5000000000 | bytes 8388608 | tf_op jit(solution)/shard_map/mixer_rest/pallas_call | solution.py:185
  43.4 29.5 %all_to_all.10.got_ref = bf16[64,8,128]{2,1,0:T(8,128)(2,1)S(1)} all-to-all(bf16[64,8,128]{2,1,0:T(8,128)(2,1)} %get-tuple-element.20), channel_id=1, replica_groups=mesh['ctx'=64,'dp'=8] {'ctx'}, dimensions={0} | all-to-all | bytes 262144 | tf_op jit(solution)/shard_map/all_to_all | solution.py:510
  72.9 0.0 copy-done.4
  72.9 0.8 prefix.1
  73.7 7.0 %all-to-all-start.1 = ((f32[64,4,128]{2,1,0:T(4,128)}), f32[64,4,128]{2,1,0:T(4,128)S(1)}, u32[]{:S(2)}, u32[]{:S(2)}) async-start(f32[64,4,128]{2,1,0:T(4,128)} %prefix.1), calls=%async_computation.1 | async-start | bytes 262144 | tf_op jit(solution)/shard_map/all_to_all | solution.py:514
  80.7 0.0 copy-start.2
  80.7 0.0 copy-start.3
  80.7 0.0 collective-permute-done.p_ref
  80.7 0.0 collective-permute-done.1.k1_ref
  80.7 0.0 collective-permute-done.2.k2_ref
  80.7 6.8 %scores.1 = (bf16[8,768,256]{2,1,0:T(8,128)(2,1)}, bf16[8,512,256]{2,1,0:T(8,128)(2,1)}, f32[32,256]{1,0:T(8,128)S(1)}) custom-call(s32[1]{0:T(128)} %bitcast.pos_ref, bf16[256,1024]{1,0:T(8,128)(2,1)} %q_ref.1, bf16[256,1024]{1,0:T(8,128)(2,1)S(1)} %collective-permute-done.p_ref, bf16[256,1024]{1,0:T(8,128)(2,1)} %k0_ref.1, ...), custom_call_target="tpu_custom_call" | custom-call | flops 700000000 | bytes 8388608 | tf_op jit(solution)/shard_map/scores/pallas_call | solution.py:414
  87.5 0.0 copy-start
  87.5 7.6 %collective-permute-start.5 = (f32[32,256]{1,0:T(8,128)S(1)}, f32[32,256]{1,0:T(8,128)S(1)}, u32[]{:S(2)}, u32[]{:S(2)}) collective-permute-start(f32[32,256]{1,0:T(8,128)S(1)} %get-tuple-element.23.stat_ref), channel_id=1, source_target_pairs={{0,8},{8,0},{16,24},{24,16},{32,40},{40,32},{48,56},{56,48},{64,72... | collective-permute-start | bytes 98312 | tf_op jit(solution)/shard_map/ppermute | solution.py:493
  95.1 0.0 collective-permute-done.4.v2_ref
  95.1 0.0 collective-permute-done.3.v1_ref
  95.1 2.5 %collective-permute-done.5.got_ref = f32[32,256]{1,0:T(8,128)S(1)} collective-permute-done((f32[32,256]{1,0:T(8,128)S(1)}, f32[32,256]{1,0:T(8,128)S(1)}, u32[]{:S(2)}, u32[]{:S(2)}) %collective-permute-start.5) | collective-permute-done | bytes 32800 | tf_op jit(solution)/shard_map/ppermute | solution.py:493
  97.6 0.0 copy-done.2
  97.6 0.0 copy-done.3
  97.6 1.6 %copy-done.1 = bf16[8,512,256]{2,1,0:T(8,128)(2,1)S(1)} copy-done((bf16[8,512,256]{2,1,0:T(8,128)(2,1)S(1)}, bf16[8,512,256]{2,1,0:T(8,128)(2,1)}, u32[]{:S(2)}) %copy-start.1) | copy-done | bytes 2097176
  99.2 3.3 %values_other.1 = bf16[128,256]{1,0:T(8,128)(2,1)S(1)} custom-call(s32[1]{0:T(128)} %bitcast.pos_ref, bf16[8,512,256]{2,1,0:T(8,128)(2,1)S(1)} %copy-done.1, bf16[256,1024]{1,0:T(8,128)(2,1)S(1)} %copy-done.2, bf16[256,1024]{1,0:T(8,128)(2,1)S(1)} %collective-permute-done.3.v1_ref, bf16[256,1024]{1,0:T(8,128)(2,1)S(1)} %collective-permute-done.4.v2_ref, ...), custom_call_target="tpu_custom_call" | custom-call | flops 400000000 | bytes 4194304 | tf_op jit(solution)/shard_map/values_other/pallas_call | solution.py:471
  102.5 7.5 %collective-permute-start.6 = (bf16[128,256]{1,0:T(8,128)(2,1)S(1)}, bf16[128,256]{1,0:T(8,128)(2,1)S(1)}, u32[]{:S(2)}, u32[]{:S(2)}) collective-permute-start(bf16[128,256]{1,0:T(8,128)(2,1)S(1)} %values_other.1), channel_id=1, source_target_pairs={{0,8},{8,0},{16,24},{24,16},{32,40},{40,32},{48,56},{56,48},{64,72... | collective-permute-start | bytes 196616 | tf_op jit(solution)/shard_map/ppermute | solution.py:493
  110.0 0.0 copy-done
  110.0 3.3 %values_own.1.own_ref = f32[128,256]{1,0:T(8,128)S(1)} custom-call(s32[1]{0:T(128)} %bitcast.pos_ref, bf16[8,768,256]{2,1,0:T(8,128)(2,1)S(1)} %copy-done, bf16[256,1024]{1,0:T(8,128)(2,1)S(1)} %copy-done.2, bf16[256,1024]{1,0:T(8,128)(2,1)S(1)} %collective-permute-done.3.v1_ref, bf16[256,1024]{1,0:T(8,128)(2,1)S(1)} %collective-permute-done.4.v2_ref, ...), custom_call_target="tpu_custom_call" | custom-call | flops 400000000 | bytes 4194304 | tf_op jit(solution)/shard_map/values_own/pallas_call | solution.py:471
  113.3 0.0 all-to-all-done.1.enter_ref
  113.3 0.0 collective-permute-done.6.back_ref
  113.4 9.8 %enter.1 = bf16[256,128]{1,0:T(8,128)(2,1)} custom-call(f32[16,16,2048]{2,1,0:T(8,128)} %get-tuple-element.18.y_ref, f32[16,16,2048]{2,1,0:T(8,128)} %get-tuple-element.19.cum_ref, f32[64,4,128]{2,1,0:T(4,128)S(1)} %all-to-all-done.1.enter_ref, f32[16,2048]{1,0:T(8,128)} %log_ref.3, bf16[16,32,256]{2,1,0:T(8,128)(2,1)} %get-tuple-element.21.out_ref, ...), custom_call_target="tpu_custom_call" | custom-call | flops 4000000000 | bytes 6291456 | tf_op jit(solution)/shard_map/enter/pallas_call | solution.py:294
  (2 shorter events, 0.0 us)
Async XLA Ops:
  0.0 80.7 %collective-permute-start.1 = (bf16[256,1024]{1,0:T(8,128)(2,1)}, bf16[256,1024]{1,0:T(8,128)(2,1)S(1)}, u32[]{:S(2)}, u32[]{:S(2)}) collective-permute-start(bf16[256,1024]{1,0:T(8,128)(2,1)} %k0_ref.1), channel_id=1, source_target_pairs={{0,16},{8,24},{16,32},{24,40},{32,48},{40,56},{48,64},{56,72},{64,... | collective-permute-start | bytes 1572872 | tf_op jit(solution)/shard_map/ppermute | solution.py:489
  3.4 77.3 %collective-permute-start.2 = (bf16[256,1024]{1,0:T(8,128)(2,1)}, bf16[256,1024]{1,0:T(8,128)(2,1)S(1)}, u32[]{:S(2)}, u32[]{:S(2)}) collective-permute-start(bf16[256,1024]{1,0:T(8,128)(2,1)} %k0_ref.1), channel_id=1, source_target_pairs={{0,32},{8,40},{16,48},{24,56},{32,64},{40,72},{48,80},{56,88},{64,... | collective-permute-start | bytes 1572872 | tf_op jit(solution)/shard_map/ppermute | solution.py:489
  7.7 87.4 %collective-permute-start.4 = (bf16[256,1024]{1,0:T(8,128)(2,1)}, bf16[256,1024]{1,0:T(8,128)(2,1)S(1)}, u32[]{:S(2)}, u32[]{:S(2)}) collective-permute-start(bf16[256,1024]{1,0:T(8,128)(2,1)} %v0_ref.3), channel_id=1, source_target_pairs={{0,32},{8,40},{16,48},{24,56},{32,64},{40,72},{48,80},{56,88},{64,... | collective-permute-start | bytes 1572872 | tf_op jit(solution)/shard_map/ppermute | solution.py:489
  11.8 83.3 %collective-permute-start.3 = (bf16[256,1024]{1,0:T(8,128)(2,1)}, bf16[256,1024]{1,0:T(8,128)(2,1)S(1)}, u32[]{:S(2)}, u32[]{:S(2)}) collective-permute-start(bf16[256,1024]{1,0:T(8,128)(2,1)} %v0_ref.3), channel_id=1, source_target_pairs={{0,16},{8,24},{16,32},{24,40},{32,48},{40,56},{48,64},{56,72},{64,... | collective-permute-start | bytes 1572872 | tf_op jit(solution)/shard_map/ppermute | solution.py:489
  15.2 65.5 %collective-permute-start = (bf16[256,1024]{1,0:T(8,128)(2,1)}, bf16[256,1024]{1,0:T(8,128)(2,1)S(1)}, u32[]{:S(2)}, u32[]{:S(2)}) collective-permute-start(bf16[256,1024]{1,0:T(8,128)(2,1)} %q_ref.1), channel_id=1, source_target_pairs={{0,8},{8,0},{16,24},{24,16},{32,40},{40,32},{48,56},{56,48},{64,72... | collective-permute-start | bytes 1572872 | tf_op jit(solution)/shard_map/ppermute | solution.py:493
  31.4 41.4 %copy-start.4 = (f32[16,2048]{1,0:T(8,128)S(1)}, f32[16,2048]{1,0:T(8,128)}, u32[]{:S(2)}) copy-start(f32[16,2048]{1,0:T(8,128)} %log_ref.3) | copy-start | bytes 393220
  73.7 39.6 %all-to-all-start.1 = ((f32[64,4,128]{2,1,0:T(4,128)}), f32[64,4,128]{2,1,0:T(4,128)S(1)}, u32[]{:S(2)}, u32[]{:S(2)}) async-start(f32[64,4,128]{2,1,0:T(4,128)} %prefix.1), calls=%async_computation.1 | async-start | bytes 262144 | tf_op jit(solution)/shard_map/all_to_all | solution.py:514
  80.7 16.9 %copy-start.2 = (bf16[256,1024]{1,0:T(8,128)(2,1)S(1)}, bf16[256,1024]{1,0:T(8,128)(2,1)}, u32[]{:S(2)}) copy-start(bf16[256,1024]{1,0:T(8,128)(2,1)} %v0_ref.3) | copy-start | bytes 1572868
  80.7 16.9 %copy-start.3 = (bf16[1024,128]{1,0:T(8,128)(2,1)S(1)}, bf16[1024,128]{1,0:T(8,128)(2,1)}, u32[]{:S(2)}) copy-start(bf16[1024,128]{1,0:T(8,128)(2,1)} %weight_ref.4) | copy-start | bytes 786436
  87.5 22.5 %copy-start = (bf16[8,768,256]{2,1,0:T(8,128)(2,1)S(1)}, bf16[8,768,256]{2,1,0:T(8,128)(2,1)}, u32[]{:S(2)}) copy-start(bf16[8,768,256]{2,1,0:T(8,128)(2,1)} %get-tuple-element.22.w_ref) | copy-start | bytes 9437188
  87.5 10.1 %collective-permute-start.5 = (f32[32,256]{1,0:T(8,128)S(1)}, f32[32,256]{1,0:T(8,128)S(1)}, u32[]{:S(2)}, u32[]{:S(2)}) collective-permute-start(f32[32,256]{1,0:T(8,128)S(1)} %get-tuple-element.23.stat_ref), channel_id=1, source_target_pairs={{0,8},{8,0},{16,24},{24,16},{32,40},{40,32},{48,56},{56,48},{64,72... | collective-permute-start | bytes 98312 | tf_op jit(solution)/shard_map/ppermute | solution.py:493
  97.6 1.6 %copy-start.1 = (bf16[8,512,256]{2,1,0:T(8,128)(2,1)S(1)}, bf16[8,512,256]{2,1,0:T(8,128)(2,1)}, u32[]{:S(2)}) copy-start(bf16[8,512,256]{2,1,0:T(8,128)(2,1)} %get-tuple-element.24.w_ref) | copy-start | bytes 6291460
  102.5 10.8 %collective-permute-start.6 = (bf16[128,256]{1,0:T(8,128)(2,1)S(1)}, bf16[128,256]{1,0:T(8,128)(2,1)S(1)}, u32[]{:S(2)}, u32[]{:S(2)}) collective-permute-start(bf16[128,256]{1,0:T(8,128)(2,1)S(1)} %values_other.1), channel_id=1, source_target_pairs={{0,8},{8,0},{16,24},{24,16},{32,40},{40,32},{48,56},{56,48},{64,72... | collective-permute-start | bytes 196616 | tf_op jit(solution)/shard_map/ppermute | solution.py:493

commit v5 on v3

--- a/solution.py
+++ b/solution.py
@@ -276,18 +276,27 @@
     )(far(y), far(cum), enter, far(decay_log), far(out_map), far(mixer_weight), own, back)
 
 
-def scores_kernel(pos_ref, q_ref, p_ref, k0_ref, k1_ref, k2_ref, away_ref, stat_ref, raw, w_ref, sems):
+def scores_kernel(
+    pos_ref, q_ref, p_ref, k0_ref, k1_ref, k2_ref, own_ref, other_ref, stat_ref, raw, w_ref, sems,
+):
     def out(h):
-        return pltpu.make_async_copy(w_ref.at[h], away_ref.at[h], sems.at[h])
+        mine = w_ref.at[h, pl.ds(0, 3 * TOK), :]
+        other = w_ref.at[h, pl.ds(3 * TOK, 2 * TOK), :]
+        return (
+            pltpu.make_async_copy(mine, own_ref.at[h], sems.at[0, h]),
+            pltpu.make_async_copy(other, other_ref.at[h], sems.at[1, h]),
+        )
 
     def head(h, carry):
         scores_head(h, pos_ref, q_ref, p_ref, k0_ref, k1_ref, k2_ref, w_ref, stat_ref, raw)
-        out(h).start()
+        for copy in out(h):
+            copy.start()
         return carry
 
     lax.fori_loop(0, HEADS, head, 0)
     for h in range(HEADS):
-        out(h).wait()
+        for copy in out(h):
+            copy.wait()
 
 
 def scores_head(h, pos_ref, q_ref, p_ref, k0_ref, k1_ref, k2_ref, w_ref, stat_ref, raw):
@@ -366,14 +375,15 @@
     return pl.pallas_call(
         scores_kernel,
         in_specs=[SMEM] + [VMEM] * 5,
-        out_specs=[AWAY, VMEM],
+        out_specs=[AWAY, AWAY, VMEM],
         scratch_shapes=[
             pltpu.VMEM((5 * TOK, TOK), F32),
             pltpu.VMEM((HEADS, 5 * TOK, TOK), BF16),
-            pltpu.SemaphoreType.DMA((HEADS,)),
+            pltpu.SemaphoreType.DMA((2, HEADS)),
         ],
         out_shape=[
-            pltpu.HBM((HEADS, 5 * TOK, TOK), BF16),
+            pltpu.HBM((HEADS, 3 * TOK, TOK), BF16),
+            pltpu.HBM((HEADS, 2 * TOK, TOK), BF16),
             jax.ShapeDtypeStruct((4 * HEADS, TOK), F32),
         ],
         compiler_params=pltpu.CompilerParams(vmem_limit_bytes=16 << 20),
@@ -381,7 +391,7 @@
             flops=700_000_000, bytes_accessed=8 << 20, transcendentals=3 << 20
         ),
         name="scores",
-    )(position, query, other, k0, k1, k2)
+    )(position, pltpu.with_memory_space_constraint(query, pltpu.HBM), other, pltpu.with_memory_space_constraint(k0, pltpu.HBM), k1, k2)
 
 
 def dot_0(a, b):
@@ -389,17 +399,9 @@
 
 
 def values_kernel(
-    mine, pos_ref, away_ref, v0_ref, v1_ref, v2_ref, stat_ref, got_ref, weight_ref, o_ref,
-    scale_s, sum_s, w_ref, sems,
+    mine, pos_ref, w_ref, v0_ref, v1_ref, v2_ref, stat_ref, got_ref, weight_ref, o_ref,
+    scale_s, sum_s,
 ):
-    rows = (0, 3 * TOK) if mine else (3 * TOK, 2 * TOK)
-
-    def fetch(h):
-        return pltpu.make_async_copy(away_ref.at[h, pl.ds(*rows), :], w_ref.at[h], sems.at[h])
-
-    ahead = 3
-    for h in range(ahead):
-        fetch(h).start()
     side = lax.rem(pos_ref[0], 2)
     at = lambda ref, k: (ref[k * 8 : k * 8 + 8, :], ref[k * 8 + 8 : k * 8 + 16, :])
     (m0, l0), (m1, l1) = at(stat_ref, 0 if mine else 2), at(got_ref, 2 if mine else 0)
@@ -413,12 +415,6 @@
         span = pl.ds(pl.multiple_of(h * HD, HD), HD)
         scale = jnp.sum(jnp.where(line == h, scale_s[...], 0.0), 0, keepdims=True)
         v0, v1, v2 = v0_ref[:, span], v1_ref[:, span], v2_ref[:, span]
-        fetch(h).wait()
-
-        @pl.when(h + ahead < HEADS)
-        def _():
-            fetch(h + ahead).start()
-
         w = lambda n: w_ref[h, n * TOK : (n + 1) * TOK, :]
         if mine:
             taken = dot_0(v0, w(0)) + dot_0(v1, w(1)) + dot_0(v2, w(2))
@@ -428,20 +424,18 @@
         sum_s[...] += dot_0(weight_ref[span, :], (taken * scale).astype(BF16))
         return carry
 
-    lax.fori_loop(0, HEADS, head, 0)
+    lax.fori_loop(0, HEADS, head, 0, unroll=4)
     o_ref[...] = sum_s[...].astype(o_ref.dtype)
 
 
 def run_values(mine, position, weights, v0, v1, v2, stats, got, attend_weight):
     return pl.pallas_call(
         functools.partial(values_kernel, mine),
-        in_specs=[SMEM, AWAY] + [VMEM] * 6,
+        in_specs=[SMEM] + [VMEM] * 7,
         out_specs=VMEM,
         scratch_shapes=[
             pltpu.VMEM((HEADS, TOK), F32),
             pltpu.VMEM((EMB, TOK), F32),
-            pltpu.VMEM((HEADS, (3 if mine else 2) * TOK, TOK), BF16),
-            pltpu.SemaphoreType.DMA((HEADS,)),
         ],
         out_shape=jax.ShapeDtypeStruct((EMB, TOK), F32 if mine else BF16),
         compiler_params=pltpu.CompilerParams(vmem_limit_bytes=16 << 20),
@@ -473,16 +467,15 @@
         step_low, step_proj, step_bias, channels, decay_log, state_maps
     )
     got = lax.all_to_all(send, "ctx", 0, 0, tiled=True)
+    w_own, w_other, stats = run_scores(position, query_rows, other, key_rows, k1, k2)
     v2 = shift(value_rows, 4)
-    weights, stats = run_scores(position, query_rows, other, key_rows, k1, k2)
     given = run_prefix(position, got, decay_log)
     enter = lax.all_to_all(given, "ctx", 0, 0, tiled=True)
     got_stats = swap(stats)
     blocks = (value_rows, v1, v2, stats, got_stats, attend_weight)
-    weights = pltpu.with_memory_space_constraint(weights, pltpu.HBM)
-    give = run_values(False, position, weights, *blocks)
+    give = run_values(False, position, w_other, *blocks)
     back = swap(give)
-    own = run_values(True, position, weights, *blocks)
+    own = run_values(True, position, w_own, *blocks)
     return run_enter(y, cum, enter, decay_log, out_map, mixer_weight, own, back)
 
 

time: 129 us -> 126 us (0.977)
  Pallas kernels: 40.9 us -> 35.3 us
  local copies, waits for them, and re-layouts: 0.03 us -> 1.62 us
    pallas_call x2, Pallas kernels: 9.25 us -> 3.42 us  [run_values(): pl.pallas_call(functools.partial(values_kernel, mine), in_specs=[SMEM] +...]
    unnamed x10, local copies, waits for them, and re-layouts: 0.03 us -> 1.62 us
  transfers between devices with their start and end apart: 9 -> 9, of which waited for: 2 -> 3; matrix products, arithmetic and copies ran while one was open for 0% -> 0% of each run, Pallas kernels for 24% -> 20%
where the time goes in v5:
time: 126 us; the launch traced here: 125 us
  starting transfers between devices  56.6 us (45%)
  Pallas kernels  35.3 us (28%)
  waiting for transfers between devices  31.7 us (25%)
  local copies, waits for them, and re-layouts  1.62 us (1%)
    all_to_all x1, waiting for transfers between devices, per_device(): got = lax.all_to_all(send, 'ctx', 0, 0, tiled=True)  28.3 us
    ppermute x3, starting transfers between devices, swap(): return lax.ppermute(value, 'ctx', [(s, s ^ 1) for s in range(N_CTX)])  25.7 us
    ppermute x4, starting transfers between devices, shift(): lax.ppermute(value, 'ctx', [(s, s + steps) for s in range(N_CTX - steps)])  15.5 us
    pallas_call x1, Pallas kernels, run_mixer(): pl.pallas_call(mixer_kernel, grid=(CH // CW,), in_specs=[fixed((TOK, 128)...  14.5 us
    pallas_call x1, Pallas kernels, run_enter(): pl.pallas_call(enter_kernel, grid=(CH // CW,), in_specs=[blocked, blocked...  9.82 us
    all_to_all x1, starting transfers between devices, per_device(): got = lax.all_to_all(send, 'ctx', 0, 0, tiled=True)  8.2 us
    all_to_all x1, starting transfers between devices, per_device(): enter = lax.all_to_all(given, 'ctx', 0, 0, tiled=True)  7.13 us
    pallas_call x1, Pallas kernels, run_scores(): pl.pallas_call(scores_kernel, in_specs=[SMEM] + [VMEM] * 5, out_specs=[AW...  6.78 us
  transfers between devices with their start and end apart: 9, of which 3 were waited for; matrix products, arithmetic and copies ran while one was open for 0% of the time, Pallas kernels for 20%

profile of v5, /device:TPU:2, one launch (start us, length us, event | category | flops | bytes accessed | tf_op | source)
XLA Modules:
  0.0 125.3 jit_solution(12361166057965198651)
XLA Ops:
  0.0 3.4 %collective-permute-start.1 = (bf16[256,1024]{1,0:T(8,128)(2,1)}, bf16[256,1024]{1,0:T(8,128)(2,1)S(1)}, u32[]{:S(2)}, u32[]{:S(2)}) collective-permute-start(bf16[256,1024]{1,0:T(8,128)(2,1)} %k0_ref.1), channel_id=1, source_target_pairs={{0,16},{8,24},{16,32},{24,40},{32,48},{40,56},{48,64},{56,72},{64,... | collective-permute-start | bytes 1572872 | tf_op jit(solution)/shard_map/ppermute | solution.py:450
  3.4 4.1 %collective-permute-start.2 = (bf16[256,1024]{1,0:T(8,128)(2,1)}, bf16[256,1024]{1,0:T(8,128)(2,1)S(1)}, u32[]{:S(2)}, u32[]{:S(2)}) collective-permute-start(bf16[256,1024]{1,0:T(8,128)(2,1)} %k0_ref.1), channel_id=1, source_target_pairs={{0,32},{8,40},{16,48},{24,56},{32,64},{40,72},{48,80},{56,88},{64,... | collective-permute-start | bytes 1572872 | tf_op jit(solution)/shard_map/ppermute | solution.py:450
  7.5 2.8 %collective-permute-start.3 = (bf16[256,1024]{1,0:T(8,128)(2,1)}, bf16[256,1024]{1,0:T(8,128)(2,1)S(1)}, u32[]{:S(2)}, u32[]{:S(2)}) collective-permute-start(bf16[256,1024]{1,0:T(8,128)(2,1)} %v0_ref.3), channel_id=1, source_target_pairs={{0,16},{8,24},{16,32},{24,40},{32,48},{40,56},{48,64},{56,72},{64,... | collective-permute-start | bytes 1572872 | tf_op jit(solution)/shard_map/ppermute | solution.py:450
  10.2 5.3 %collective-permute-start.4 = (bf16[256,1024]{1,0:T(8,128)(2,1)}, bf16[256,1024]{1,0:T(8,128)(2,1)S(1)}, u32[]{:S(2)}, u32[]{:S(2)}) collective-permute-start(bf16[256,1024]{1,0:T(8,128)(2,1)} %v0_ref.3), channel_id=1, source_target_pairs={{0,32},{8,40},{16,48},{24,56},{32,64},{40,72},{48,80},{56,88},{64,... | collective-permute-start | bytes 1572872 | tf_op jit(solution)/shard_map/ppermute | solution.py:450
  15.5 10.9 %collective-permute-start = (bf16[256,1024]{1,0:T(8,128)(2,1)}, bf16[256,1024]{1,0:T(8,128)(2,1)S(1)}, u32[]{:S(2)}, u32[]{:S(2)}) collective-permute-start(bf16[256,1024]{1,0:T(8,128)(2,1)} %q_ref.1), channel_id=1, source_target_pairs={{0,8},{8,0},{16,24},{24,16},{32,40},{40,32},{48,56},{56,48},{64,72... | collective-permute-start | bytes 1572872 | tf_op jit(solution)/shard_map/ppermute | solution.py:454
  26.5 0.0 copy-start.4
  26.5 14.5 %mixer.1 = (f32[16,16,2048]{2,1,0:T(8,128)}, f32[16,16,2048]{2,1,0:T(8,128)}, bf16[64,8,128]{2,1,0:T(8,128)(2,1)}, bf16[16,32,256]{2,1,0:T(8,128)(2,1)}) custom-call(bf16[256,128]{1,0:T(8,128)(2,1)} %low_ref.1, bf16[128,2048]{1,0:T(8,128)(2,1)} %proj_ref.1, f32[1,2048]{1,0:T(1,128)} %bitcast.2, bf16[256,2048]{1,0:T(8,128)(2,1)} %chan_ref.1, ...), custom_call_target="tpu_custom_call" | custom-call | flops 6000000000 | bytes 8388608 | tf_op jit(solution)/shard_map/mixer/pallas_call | solution.py:142
  40.9 8.2 %all-to-all-start = ((bf16[64,8,128]{2,1,0:T(8,128)(2,1)}), bf16[64,8,128]{2,1,0:T(8,128)(2,1)S(1)}, u32[]{:S(2)}, u32[]{:S(2)}) async-start(bf16[64,8,128]{2,1,0:T(8,128)(2,1)} %get-tuple-element.14), calls=%async_computation | async-start | bytes 262144 | tf_op jit(solution)/shard_map/all_to_all | solution.py:469
  49.1 28.3 %all-to-all-done.got_ref = bf16[64,8,128]{2,1,0:T(8,128)(2,1)S(1)} async-done(((bf16[64,8,128]{2,1,0:T(8,128)(2,1)}), bf16[64,8,128]{2,1,0:T(8,128)(2,1)S(1)}, u32[]{:S(2)}, u32[]{:S(2)}) %all-to-all-start) | async-done | bytes 131104 | tf_op jit(solution)/shard_map/all_to_all | solution.py:469
  77.4 0.0 copy-done.4
  77.4 0.8 prefix.1
  78.2 7.1 %all-to-all-start.1 = ((f32[64,4,128]{2,1,0:T(4,128)}), f32[64,4,128]{2,1,0:T(4,128)S(1)}, u32[]{:S(2)}, u32[]{:S(2)}) async-start(f32[64,4,128]{2,1,0:T(4,128)} %prefix.1), calls=%async_computation.1 | async-start | bytes 262144 | tf_op jit(solution)/shard_map/all_to_all | solution.py:473
  85.4 0.0 copy-start.2
  85.4 0.0 copy-start.3
  85.4 0.0 collective-permute-done.p_ref
  85.4 0.0 collective-permute-done.1.k1_ref
  85.4 0.0 collective-permute-done.2.k2_ref
  85.4 6.8 %scores.1 = (bf16[8,768,256]{2,1,0:T(8,128)(2,1)}, bf16[8,512,256]{2,1,0:T(8,128)(2,1)}, f32[32,256]{1,0:T(8,128)S(1)}) custom-call(s32[1]{0:T(128)} %bitcast.1.pos_ref, bf16[256,1024]{1,0:T(8,128)(2,1)} %q_ref.1, bf16[256,1024]{1,0:T(8,128)(2,1)S(1)} %collective-permute-done.p_ref, bf16[256,1024]{1,0:T(8,128)(2,1)} %k0_ref.1, ...), custom_call_target="tpu_custom_call" | custom-call | flops 700000000 | bytes 8388608 | tf_op jit(solution)/shard_map/scores/pallas_call | solution.py:375
  92.2 0.0 copy-start
  92.2 7.5 %collective-permute-start.5 = (f32[32,256]{1,0:T(8,128)S(1)}, f32[32,256]{1,0:T(8,128)S(1)}, u32[]{:S(2)}, u32[]{:S(2)}) collective-permute-start(f32[32,256]{1,0:T(8,128)S(1)} %get-tuple-element.17.stat_ref), channel_id=1, source_target_pairs={{0,8},{8,0},{16,24},{24,16},{32,40},{40,32},{48,56},{56,48},{64,72... | collective-permute-start | bytes 98312 | tf_op jit(solution)/shard_map/ppermute | solution.py:454
  99.8 0.0 collective-permute-done.3.v1_ref
  99.8 0.0 collective-permute-done.4.v2_ref
  99.8 2.5 %collective-permute-done.5.got_ref = f32[32,256]{1,0:T(8,128)S(1)} collective-permute-done((f32[32,256]{1,0:T(8,128)S(1)}, f32[32,256]{1,0:T(8,128)S(1)}, u32[]{:S(2)}, u32[]{:S(2)}) %collective-permute-start.5) | collective-permute-done | bytes 32800 | tf_op jit(solution)/shard_map/ppermute | solution.py:454
  102.3 0.0 copy-done.2
  102.3 0.0 copy-done.3
  102.3 1.6 %copy-done.1 = bf16[8,512,256]{2,1,0:T(8,128)(2,1)S(1)} copy-done((bf16[8,512,256]{2,1,0:T(8,128)(2,1)S(1)}, bf16[8,512,256]{2,1,0:T(8,128)(2,1)}, u32[]{:S(2)}) %copy-start.1) | copy-done | bytes 2097176
  103.9 1.5 %values_other.1 = bf16[128,256]{1,0:T(8,128)(2,1)S(1)} custom-call(s32[1]{0:T(128)} %bitcast.1.pos_ref, bf16[8,512,256]{2,1,0:T(8,128)(2,1)S(1)} %copy-done.1, bf16[256,1024]{1,0:T(8,128)(2,1)S(1)} %copy-done.2, bf16[256,1024]{1,0:T(8,128)(2,1)S(1)} %collective-permute-done.3.v1_ref, bf16[256,1024]{1,0:T(8,128)(2,1)S(1)} %collective-permute-done.4.v2_ref, ...), custom_call_target="tpu_custom_call" | custom-call | flops 400000000 | bytes 4194304 | tf_op jit(solution)/shard_map/values_other/pallas_call | solution.py:432
  105.4 7.3 %collective-permute-start.6 = (bf16[128,256]{1,0:T(8,128)(2,1)S(1)}, bf16[128,256]{1,0:T(8,128)(2,1)S(1)}, u32[]{:S(2)}, u32[]{:S(2)}) collective-permute-start(bf16[128,256]{1,0:T(8,128)(2,1)S(1)} %values_other.1), channel_id=1, source_target_pairs={{0,8},{8,0},{16,24},{24,16},{32,40},{40,32},{48,56},{56,48},{64,72... | collective-permute-start | bytes 196616 | tf_op jit(solution)/shard_map/ppermute | solution.py:454
  112.7 1.9 %values_own.1.own_ref = f32[128,256]{1,0:T(8,128)S(1)} custom-call(s32[1]{0:T(128)} %bitcast.1.pos_ref, bf16[8,768,256]{2,1,0:T(8,128)(2,1)S(1)} %copy-done, bf16[256,1024]{1,0:T(8,128)(2,1)S(1)} %copy-done.2, bf16[256,1024]{1,0:T(8,128)(2,1)S(1)} %collective-permute-done.3.v1_ref, bf16[256,1024]{1,0:T(8,128)(2,1)S(1)} %collective-permute-done.4.v2_ref, ...), custom_call_target="tpu_custom_call" | custom-call | flops 400000000 | bytes 4194304 | tf_op jit(solution)/shard_map/values_own/pallas_call | solution.py:432
  114.6 0.0 all-to-all-done.1.enter_ref
  114.6 0.9 collective-permute-done.6.back_ref
  115.5 9.8 %enter.1 = bf16[256,128]{1,0:T(8,128)(2,1)} custom-call(f32[16,16,2048]{2,1,0:T(8,128)} %get-tuple-element.12.y_ref, f32[16,16,2048]{2,1,0:T(8,128)} %get-tuple-element.13.cum_ref, f32[64,4,128]{2,1,0:T(4,128)S(1)} %all-to-all-done.1.enter_ref, f32[16,2048]{1,0:T(8,128)} %log_ref.5, bf16[16,32,256]{2,1,0:T(8,128)(2,1)} %get-tuple-element.15.out_ref, ...), custom_call_target="tpu_custom_call" | custom-call | flops 4000000000 | bytes 6291456 | tf_op jit(solution)/shard_map/enter/pallas_call | solution.py:255
  (2 shorter events, 0.0 us)
Async XLA Ops:
  0.0 85.4 %collective-permute-start.1 = (bf16[256,1024]{1,0:T(8,128)(2,1)}, bf16[256,1024]{1,0:T(8,128)(2,1)S(1)}, u32[]{:S(2)}, u32[]{:S(2)}) collective-permute-start(bf16[256,1024]{1,0:T(8,128)(2,1)} %k0_ref.1), channel_id=1, source_target_pairs={{0,16},{8,24},{16,32},{24,40},{32,48},{40,56},{48,64},{56,72},{64,... | collective-permute-start | bytes 1572872 | tf_op jit(solution)/shard_map/ppermute | solution.py:450
  3.4 82.0 %collective-permute-start.2 = (bf16[256,1024]{1,0:T(8,128)(2,1)}, bf16[256,1024]{1,0:T(8,128)(2,1)S(1)}, u32[]{:S(2)}, u32[]{:S(2)}) collective-permute-start(bf16[256,1024]{1,0:T(8,128)(2,1)} %k0_ref.1), channel_id=1, source_target_pairs={{0,32},{8,40},{16,48},{24,56},{32,64},{40,72},{48,80},{56,88},{64,... | collective-permute-start | bytes 1572872 | tf_op jit(solution)/shard_map/ppermute | solution.py:450
  7.5 92.3 %collective-permute-start.3 = (bf16[256,1024]{1,0:T(8,128)(2,1)}, bf16[256,1024]{1,0:T(8,128)(2,1)S(1)}, u32[]{:S(2)}, u32[]{:S(2)}) collective-permute-start(bf16[256,1024]{1,0:T(8,128)(2,1)} %v0_ref.3), channel_id=1, source_target_pairs={{0,16},{8,24},{16,32},{24,40},{32,48},{40,56},{48,64},{56,72},{64,... | collective-permute-start | bytes 1572872 | tf_op jit(solution)/shard_map/ppermute | solution.py:450
  10.2 89.5 %collective-permute-start.4 = (bf16[256,1024]{1,0:T(8,128)(2,1)}, bf16[256,1024]{1,0:T(8,128)(2,1)S(1)}, u32[]{:S(2)}, u32[]{:S(2)}) collective-permute-start(bf16[256,1024]{1,0:T(8,128)(2,1)} %v0_ref.3), channel_id=1, source_target_pairs={{0,32},{8,40},{16,48},{24,56},{32,64},{40,72},{48,80},{56,88},{64,... | collective-permute-start | bytes 1572872 | tf_op jit(solution)/shard_map/ppermute | solution.py:450
  15.5 69.9 %collective-permute-start = (bf16[256,1024]{1,0:T(8,128)(2,1)}, bf16[256,1024]{1,0:T(8,128)(2,1)S(1)}, u32[]{:S(2)}, u32[]{:S(2)}) collective-permute-start(bf16[256,1024]{1,0:T(8,128)(2,1)} %q_ref.1), channel_id=1, source_target_pairs={{0,8},{8,0},{16,24},{24,16},{32,40},{40,32},{48,56},{56,48},{64,72... | collective-permute-start | bytes 1572872 | tf_op jit(solution)/shard_map/ppermute | solution.py:454
  26.5 51.0 %copy-start.4 = (f32[16,2048]{1,0:T(8,128)S(1)}, f32[16,2048]{1,0:T(8,128)}, u32[]{:S(2)}) copy-start(f32[16,2048]{1,0:T(8,128)} %log_ref.5) | copy-start | bytes 393220
  40.9 36.5 %all-to-all-start = ((bf16[64,8,128]{2,1,0:T(8,128)(2,1)}), bf16[64,8,128]{2,1,0:T(8,128)(2,1)S(1)}, u32[]{:S(2)}, u32[]{:S(2)}) async-start(bf16[64,8,128]{2,1,0:T(8,128)(2,1)} %get-tuple-element.14), calls=%async_computation | async-start | bytes 262144 | tf_op jit(solution)/shard_map/all_to_all | solution.py:469
  78.2 36.4 %all-to-all-start.1 = ((f32[64,4,128]{2,1,0:T(4,128)}), f32[64,4,128]{2,1,0:T(4,128)S(1)}, u32[]{:S(2)}, u32[]{:S(2)}) async-start(f32[64,4,128]{2,1,0:T(4,128)} %prefix.1), calls=%async_computation.1 | async-start | bytes 262144 | tf_op jit(solution)/shard_map/all_to_all | solution.py:473
  85.4 16.9 %copy-start.2 = (bf16[256,1024]{1,0:T(8,128)(2,1)S(1)}, bf16[256,1024]{1,0:T(8,128)(2,1)}, u32[]{:S(2)}) copy-start(bf16[256,1024]{1,0:T(8,128)(2,1)} %v0_ref.3) | copy-start | bytes 1572868
  85.4 16.9 %copy-start.3 = (bf16[1024,128]{1,0:T(8,128)(2,1)S(1)}, bf16[1024,128]{1,0:T(8,128)(2,1)}, u32[]{:S(2)}) copy-start(bf16[1024,128]{1,0:T(8,128)(2,1)} %weight_ref.4) | copy-start | bytes 786436
  92.2 20.5 %copy-start = (bf16[8,768,256]{2,1,0:T(8,128)(2,1)S(1)}, bf16[8,768,256]{2,1,0:T(8,128)(2,1)}, u32[]{:S(2)}) copy-start(bf16[8,768,256]{2,1,0:T(8,128)(2,1)} %get-tuple-element.16.w_ref) | copy-start | bytes 9437188
  92.2 10.1 %collective-permute-start.5 = (f32[32,256]{1,0:T(8,128)S(1)}, f32[32,256]{1,0:T(8,128)S(1)}, u32[]{:S(2)}, u32[]{:S(2)}) collective-permute-start(f32[32,256]{1,0:T(8,128)S(1)} %get-tuple-element.17.stat_ref), channel_id=1, source_target_pairs={{0,8},{8,0},{16,24},{24,16},{32,40},{40,32},{48,56},{56,48},{64,72... | collective-permute-start | bytes 98312 | tf_op jit(solution)/shard_map/ppermute | solution.py:454
  102.3 1.6 %copy-start.1 = (bf16[8,512,256]{2,1,0:T(8,128)(2,1)S(1)}, bf16[8,512,256]{2,1,0:T(8,128)(2,1)}, u32[]{:S(2)}) copy-start(bf16[8,512,256]{2,1,0:T(8,128)(2,1)} %get-tuple-element.18.w_ref) | copy-start | bytes 6291460
  105.4 10.1 %collective-permute-start.6 = (bf16[128,256]{1,0:T(8,128)(2,1)S(1)}, bf16[128,256]{1,0:T(8,128)(2,1)S(1)}, u32[]{:S(2)}, u32[]{:S(2)}) collective-permute-start(bf16[128,256]{1,0:T(8,128)(2,1)S(1)} %values_other.1), channel_id=1, source_target_pairs={{0,8},{8,0},{16,24},{24,16},{32,40},{40,32},{48,56},{56,48},{64,72... | collective-permute-start | bytes 196616 | tf_op jit(solution)/shard_map/ppermute | solution.py:454
